TPU v7x, 32 devices: a whole 2x2x4 slice. The times are simulated.
32 devices in a mesh: row: 4 (over y, core), col: 2 (over x), depth: 4 (over z).
Axes of the slice: x: 2, y: 2, z: 4, core: 2. Of those that a mesh axis runs over, the one named last changes fastest.
Arguments:
- density: float32 [512, 5, 128, 128], P(('row', 'depth'), None, 'col'), may hold values from -0.6 to 0.6
- pattern: int32 [512, 5], P(('row', 'depth')), may hold values 0 or 1
Outputs:
- purified: float32 [512, 5, 128, 128], P(('row', 'depth'), None, 'col')
All inputs are finite; a program needn't handle non-finite values. No bound on the sum of `pattern` on one device may be relied on, other than what follows from the above.
Results may differ from a plain program's by a relative error of at most 0.0001.
Values sent between devices are 32-bit elements; how exact they have to be, the bound alone decides.
A program may use at most 64 MiB of HBM per device.

v0:
```python
import functools

import jax
import jax.numpy as jnp
from jax import lax
from jax.experimental import pallas as pl
from jax.experimental.pallas import tpu as pltpu
from jax.sharding import PartitionSpec as P

MESH = pl.DeviceIdType.MESH
WIDE = 5
SLOTS = 6
RING = ("row", "depth")


def split(value):
    high = value.astype(jnp.bfloat16)
    low = (value - high.astype(jnp.float32)).astype(jnp.bfloat16)
    return high, low


def dot(a, b):
    return jnp.dot(a, b, preferred_element_type=jnp.float32)


def products(block, h, me, masks, high, low, out):
    two = 2 * block

    def product(j, a, b, sources=(0, 1, 2), start=None):
        both = jnp.concatenate([a, b], axis=0)
        m = a.shape[0]
        parts = []
        for n in range(3):
            total = None if start is None else start[:, n * two:(n + 1) * two]
            for k in sources:
                at = n - k + 1
                if at < 0 or at > 2:
                    continue
                lanes = slice(at * two, (at + 1) * two)
                ks = slice(k * two, (k + 1) * two)
                stacked = dot(both[:, ks], high[j + k - 1, :, lanes])
                term = stacked[:m] + stacked[m:] + dot(a[:, ks], low[j + k - 1, :, lanes])
                total = term if total is None else total + term
            parts.append(total)
        return jnp.concatenate(parts, axis=1)

    def own_rows(ref, j):
        return jnp.concatenate(
            [ref[j, pl.ds(pl.multiple_of(p * block + me * h, h), h), :] for p in range(2)], axis=0)

    def compute(j, to, sources=(0, 1, 2), start=None):
        factor = jnp.concatenate(
            [jnp.broadcast_to(masks[j, p:p + 1, :], (h, SLOTS * block)) for p in range(2)], axis=0)
        square = product(j, own_rows(high, j), own_rows(low, j), sources, start) * factor
        cube = product(j, *split(square)) * factor
        value = 3.0 * square - 2.0 * cube
        for p in range(2):
            for s in range(WIDE):
                out[to, p, s] = value[p * h:(p + 1) * h, (p + s) * block:(p + s + 1) * block]

    return product, own_rows, compute


BEFORE = ((0, 1), (0, 2), (1, 2))
AFTER = ((2,), (1,), (0,))
LATE = 3


def finish(masks, high, low, early, begun, out, late, early_sem, late_sem):
    count, h, block = early.shape[0], early.shape[3], early.shape[4]
    me = lax.axis_index("col")
    first = pltpu.make_async_copy(early, out.at[pl.ds(0, count)], early_sem)
    first.start()
    _, _, compute = products(block, h, me, masks, high, low, late)

    def result(i):
        return pltpu.make_async_copy(late.at[i], out.at[count + i], late_sem.at[i])

    for i in range(LATE):
        compute(count + 1 + i, i, AFTER[i], begun[i])
        result(i).start()

    first.wait()

    @pl.loop(0, LATE)
    def _(i):
        result(i).wait()


def kernel(cols, ring, dens, pattern, masks, high, low, early, begun, raw, flags,
           local_sem, flag_sem, send_sem, recv_sem, edge_send, edge_recv,
           relay_send, relay_recv, flag_send, flag_recv, up, down, corner):
    pairs = dens.shape[0]
    h = dens.shape[3]
    block = dens.shape[4]
    last = pairs + 1
    me = lax.axis_index("col")
    depth = lax.axis_size("depth")
    place = lax.axis_index("row") * depth + lax.axis_index("depth")

    def on_ring(shift):
        at = lax.rem(place + shift + ring, ring)
        return {"row": at // depth, "depth": lax.rem(at, depth)}

    prev, following = on_ring(-1), on_ring(1)

    def peer(step):
        return {"col": lax.rem(me + step, cols)}

    def source(step):
        return lax.rem(me + cols - step, cols)

    def own(j):
        return pltpu.make_async_copy(dens.at[j - 1], raw.at[me, j], local_sem.at[j - 1])

    def across(step, j):
        return pltpu.make_async_remote_copy(
            dens.at[j - 1], raw.at[me, j], send_sem.at[step - 1, j - 1],
            recv_sem.at[step - 1, j - 1], device_id=peer(step), device_id_type=MESH)

    ends = ((pairs, 0, following), (1, last, prev))

    def edge(side):
        j, slot, device = ends[side]
        return pltpu.make_async_remote_copy(
            dens.at[j - 1], raw.at[me, slot], edge_send.at[side], edge_recv.at[side],
            device_id=device, device_id_type=MESH)

    def relay(side, step):
        j, slot, device = ends[side]
        return pltpu.make_async_remote_copy(
            raw.at[source(step), j], raw.at[source(step), slot], relay_send.at[side, step - 1],
            relay_recv.at[side, step - 1], device_id=device, device_id_type=MESH)

    def flag_edge(side):
        return pltpu.make_async_remote_copy(
            pattern, flags.at[2 * side], flag_send.at[side], flag_recv.at[side],
            device_id=ends[side][2], device_id_type=MESH)

    steps = range(1, cols)

    z, r = lax.axis_index("depth"), lax.axis_index("row")
    row_count = lax.axis_size("row")

    def greet(semaphore, device):
        pl.semaphore_signal(semaphore, inc=1, device_id=device, device_id_type=MESH)

    def along(step):
        return {"depth": z + step}

    def beside(step):
        return {"row": lax.rem(r + step + row_count, row_count)}

    barrier = pltpu.get_barrier_semaphore()
    for s in steps:
        greet(barrier, peer(s))

    @pl.when(z > 0)
    def _():
        greet(barrier, along(-1))

    @pl.when(z < depth - 1)
    def _():
        greet(barrier, along(1))

    @pl.when(z == 0)
    def _():
        greet(barrier, beside(-1))
        greet(barrier, beside(1))

    own_flags = pltpu.make_async_copy(pattern, flags.at[1], flag_sem)
    own_flags.start()
    near = jnp.where(z == 0, 2, 1) + jnp.where(z < depth - 1, 1, 0)
    pl.semaphore_wait(barrier, cols - 1 + near)

    for j in (1, pairs):
        for s in steps:
            across(s, j).start()

    @pl.loop(2, pairs)
    def _(j):
        for s in steps:
            across(s, j).start()

    @pl.when(z > 0)
    def _():
        pl.semaphore_wait(up, 1)

    @pl.when(z < depth - 1)
    def _():
        greet(up, along(1))

    @pl.when(z < depth - 2)
    def _():
        pl.semaphore_wait(down, 1)

    @pl.when((z > 0) & (z <= depth - 2))
    def _():
        greet(down, along(-1))

    @pl.when(z == 0)
    def _():
        greet(corner, beside(1))
        pl.semaphore_wait(corner, 1)

    for side in (0, 1):
        flag_edge(side).start()
        edge(side).start()

    @pl.loop(1, pairs + 1)
    def _(j):
        own(j).start()

    def expand(which, i, j):
        lane = lax.broadcasted_iota(jnp.int32, flags.shape[1:], 1)
        for p in range(2):
            picked = jnp.where(lane == i + p, flags[which], 0).astype(jnp.float32)
            spread = jnp.broadcast_to(jnp.sum(picked, axis=1, keepdims=True), (WIDE, block))
            for s in range(WIDE):
                masks[j, p:p + 1, (p + s) * block:(p + s + 1) * block] = spread[s:s + 1]
            empty = slice(0, block) if p else slice(WIDE * block, SLOTS * block)
            masks[j, p:p + 1, empty] = jnp.zeros((1, block), jnp.float32)

    def convert(j):
        for p in range(2):
            for s in range(WIDE):
                slot = p + s
                factor = masks[j, p:p + 1, slot * block:(slot + 1) * block]
                for c in range(cols):
                    a, b = split(raw[c, j, p, s] * factor)
                    rows = slice(p * block + c * h, p * block + (c + 1) * h)
                    lanes = slice(slot * block, (slot + 1) * block)
                    high[j, rows, lanes] = a
                    low[j, rows, lanes] = b
            empty = slice(0, block) if p else slice(WIDE * block, SLOTS * block)
            nothing = jnp.zeros((block, block), jnp.bfloat16)
            high[j, p * block:(p + 1) * block, empty] = nothing
            low[j, p * block:(p + 1) * block, empty] = nothing

    product, own_rows, compute = products(block, h, me, masks, high, low, early)

    own_flags.wait()

    @pl.loop(1, pairs + 1)
    def _(j):
        expand(1, 2 * (j - 1), j)

    for side in (0, 1):
        flag_edge(side).wait_recv()
    expand(0, 2 * (pairs - 1), 0)
    expand(2, 0, last)

    @pl.loop(1, pairs + 1)
    def _(j):
        own(j).wait()

    for j, side in ((1, 1), (pairs, 0)):
        for s in steps:
            across(s, j).wait_recv()
            relay(side, s).start()
        convert(j)
    for side in (0, 1):
        edge(side).wait_recv()
        for s in steps:
            relay(side, s).wait_recv()
        convert(ends[side][1])

    @pl.loop(2, pairs - 1)
    def _(j):
        for s in steps:
            across(s, j).wait_recv()
        convert(j)
        compute(j - 1, j - 2)

    def local_rows(j):
        rows = []
        for p in range(2):
            blocks = [raw[me, j, p, s] for s in range(WIDE)]
            empty = [jnp.zeros((h, block), jnp.float32)]
            row = jnp.concatenate(empty + blocks if p else blocks + empty, axis=1)
            rows.append(row * masks[j, p:p + 1, :])
        return split(jnp.concatenate(rows, axis=0))

    for i in range(LATE):
        j = pairs - LATE + 1 + i
        a, b = local_rows(j) if i == 1 else (own_rows(high, j), own_rows(low, j))
        begun[i] = product(j, a, b, BEFORE[i])

    for side in (0, 1):
        flag_edge(side).wait_send()
        edge(side).wait_send()
        for s in steps:
            relay(side, s).wait_send()
    for s in steps:
        across(s, pairs - 1).wait_recv()
    convert(pairs - 1)

    @pl.loop(1, pairs + 1)
    def _(j):
        for s in steps:
            across(s, j).wait_send()


def shards(cols, ring, density, pattern):
    rows, wide, h, block = density.shape
    pairs = rows // 2
    paired = density.reshape(pairs, 2, wide, h, block)
    width = SLOTS * block
    dma = pltpu.SemaphoreType.DMA
    vmem = pl.BlockSpec(memory_space=pltpu.VMEM)
    held = pl.pallas_call(
        functools.partial(kernel, cols, ring),
        out_shape=[
            pltpu.VMEM((pairs + 2, 8, width), jnp.float32),
            pltpu.VMEM((pairs + 2, 2 * block, width), jnp.bfloat16),
            pltpu.VMEM((pairs + 2, 2 * block, width), jnp.bfloat16),
            pltpu.VMEM((pairs - LATE,) + paired.shape[1:], jnp.float32),
            pltpu.VMEM((LATE, 2 * h, width), jnp.float32),
        ],
        in_specs=[pl.BlockSpec(memory_space=pltpu.HBM)] * 2,
        out_specs=[vmem] * 5,
        scratch_shapes=[
            pltpu.VMEM((cols, pairs + 2, 2, wide, h, block), jnp.float32),
            pltpu.VMEM((3, wide, rows), jnp.int32),
            dma((pairs,)),
            dma,
            dma((cols - 1, pairs)),
            dma((cols - 1, pairs)),
            dma((2,)),
            dma((2,)),
            dma((2, cols - 1)),
            dma((2, cols - 1)),
            dma((2,)),
            dma((2,)),
            pltpu.SemaphoreType.REGULAR,
            pltpu.SemaphoreType.REGULAR,
            pltpu.SemaphoreType.REGULAR,
        ],
        compiler_params=pltpu.CompilerParams(
            collective_id=0, has_side_effects=True, vmem_limit_bytes=42 << 20),
    )(*(pltpu.with_memory_space_constraint(x, pltpu.HBM) for x in (paired, pattern.T)))
    out = pl.pallas_call(
        finish,
        out_shape=jax.ShapeDtypeStruct(paired.shape, jnp.float32),
        in_specs=[vmem] * 5,
        out_specs=pl.BlockSpec(memory_space=pltpu.HBM),
        scratch_shapes=[
            pltpu.VMEM((LATE,) + paired.shape[1:], jnp.float32),
            dma,
            dma((LATE,)),
        ],
        compiler_params=pltpu.CompilerParams(vmem_limit_bytes=16 << 20),
    )(*held)
    return out.reshape(density.shape)


def solution(mesh):
    cols = mesh.shape["col"]
    ring = mesh.shape["row"] * mesh.shape["depth"]
    in_specs = (P(RING, None, "col", None), P(RING, None))
    out_specs = P(RING, None, "col", None)
    body = functools.partial(shards, cols, ring)
    return jax.shard_map(body, mesh=mesh, in_specs=in_specs, out_specs=out_specs, check_vma=False)
```

profile of v0, /device:TPU:0, one launch (start us, length us, event | category | flops | bytes accessed | tf_op | source)
XLA Modules:
  0.0 121.3 jit_solution(555815792851718887)
XLA Ops:
  0.0 118.8 %shard_map.28 = (f32[18,8,768]{2,1,0:T(8,128)S(1)}, bf16[18,256,768]{2,1,0:T(8,128)(2,1)S(1)}, bf16[18,256,768]{2,1,0:T(8,128)(2,1)S(1)}, f32[13,2,5,64,128]{4,3,2,1,0:T(8,128)S(1)}, f32[3,128,768]{2,1,0:T(8,128)S(1)}) custom-call(f32[16,2,5,64,128]{4,3,2,1,0:T(8,128)} %bitcast.3, s32[5,32]{1,0:T(8,128)} %bitcast.4), custom_call_target="tpu_custom_call" | custom-call | tf_op jit(solution)/shard_map/pallas_call | solution.py:311
  118.8 2.5 %shard_map.29 = f32[16,2,5,64,128]{4,3,2,1,0:T(8,128)} custom-call(f32[18,8,768]{2,1,0:T(8,128)S(1)} %get-tuple-element.10.masks, bf16[18,256,768]{2,1,0:T(8,128)(2,1)S(1)} %get-tuple-element.11.high, bf16[18,256,768]{2,1,0:T(8,128)(2,1)S(1)} %get-tuple-element.12.low, f32[13,2,5,64,128]{4,3,2,1,0:T(8,128)S(1)} %get-tuple-element.13.early, ...), custom_call_target="tpu_custom_call" | custom-call | tf_op jit(solution)/shard_map/pallas_call | solution.py:342
where the time goes:
time: 121 us
  Pallas kernels  121 us (100%)
    pallas_call x1, Pallas kernels, shards(): pl.pallas_call(functools.partial(kernel, cols, ring), out_shape=[pltpu.VM...  119 us
    pallas_call x1, Pallas kernels, shards(): pl.pallas_call(finish, out_shape=jax.ShapeDtypeStruct(paired.shape, jnp.f...  2.46 us

commit v1 on v0

--- a/solution.py
+++ b/solution.py
@@ -66,28 +66,35 @@
 LATE = 3
 
 
-def finish(masks, high, low, early, begun, out, late, early_sem, late_sem):
-    count, h, block = early.shape[0], early.shape[3], early.shape[4]
+def finish(first_late, masks, high, low, early, begun, out, late, early_sem, late_sem):
+    h, block = early.shape[3], early.shape[4]
     me = lax.axis_index("col")
-    first = pltpu.make_async_copy(early, out.at[pl.ds(0, count)], early_sem)
-    first.start()
+    before = first_late - 1
+    after = early.shape[0] - before
+    firsts = [pltpu.make_async_copy(early.at[pl.ds(0, before)], out.at[pl.ds(0, before)], early_sem.at[0])]
+    if after:
+        firsts.append(pltpu.make_async_copy(
+            early.at[pl.ds(before, after)], out.at[pl.ds(before + LATE, after)], early_sem.at[1]))
+    for first in firsts:
+        first.start()
     _, _, compute = products(block, h, me, masks, high, low, late)
 
     def result(i):
-        return pltpu.make_async_copy(late.at[i], out.at[count + i], late_sem.at[i])
+        return pltpu.make_async_copy(late.at[i], out.at[before + i], late_sem.at[i])
 
     for i in range(LATE):
-        compute(count + 1 + i, i, AFTER[i], begun[i])
+        compute(first_late + i, i, AFTER[i], begun[i])
         result(i).start()
 
-    first.wait()
+    for first in firsts:
+        first.wait()
 
     @pl.loop(0, LATE)
     def _(i):
         result(i).wait()
 
 
-def kernel(cols, ring, dens, pattern, masks, high, low, early, begun, raw, flags,
+def dense_kernel(cols, ring, dens, pattern, masks, high, low, early, begun, raw, flags,
            local_sem, flag_sem, send_sem, recv_sem, edge_send, edge_recv,
            relay_send, relay_recv, flag_send, flag_recv, up, down, corner):
     pairs = dens.shape[0]
@@ -301,57 +308,480 @@
             across(s, j).wait_send()
 
 
-def shards(cols, ring, density, pattern):
+GUEST = 2
+
+
+def sparse_kernel(ring, dens, pattern, masks, high, low, early, begun, over,
+                  mine, theirs, hosted, guests, flags, bits, queue, hole, place_of,
+                  local_sem, guest_sem, flag_sem, bits_sem, send_sem, recv_sem, edge_send, edge_recv,
+                  relay_send, relay_recv, flag_send, flag_recv, up, down, corner):
+    pairs, pair_slots, h, block = dens.shape
+    last = pairs + 1
+    first_guest = pairs - GUEST
+    tail = first_guest - 1
+    room = guests.shape[0]
+    hosts = hosted.shape[0]
+    me = lax.axis_index("col")
+    depth = lax.axis_size("depth")
+    place = lax.axis_index("row") * depth + lax.axis_index("depth")
+
+    def on_ring(shift):
+        at = lax.rem(place + shift + ring, ring)
+        return {"row": at // depth, "depth": lax.rem(at, depth)}
+
+    prev, following = on_ring(-1), on_ring(1)
+    peer = {"col": 1 - me}
+
+    def own(j):
+        return pltpu.make_async_copy(dens.at[j - 1], mine.at[j], local_sem.at[j - 1])
+
+    def own_guest(i):
+        return pltpu.make_async_copy(
+            dens.at[first_guest - 1 + i], guests.at[pl.ds(i * pair_slots, pair_slots)], guest_sem.at[i])
+
+    def crossing(source, target, n):
+        return pltpu.make_async_remote_copy(
+            source, target, send_sem.at[n], recv_sem.at[n], device_id=peer, device_id_type=MESH)
+
+    def at_host(j):
+        return pl.ds((j - 1) * pair_slots, pair_slots)
+
+    def across(j):
+        return crossing(mine.at[j], hosted.at[at_host(j)], j)
+
+    across_first = crossing(dens.at[0], theirs.at[1], 1)
+    across_last = crossing(mine.at[pairs], hosted.at[pl.ds(0, pair_slots)], 0)
+    half_host = pl.ds((tail - 1) * pair_slots, WIDE)
+    across_half = crossing(mine.at[tail, pl.ds(0, WIDE)], hosted.at[half_host], tail)
+    across_end = crossing(
+        dens.at[tail - 1, pl.ds(WIDE, WIDE)], theirs.at[3, pl.ds(WIDE, WIDE)], tail + 1)
+
+    ends = ((pairs, 0, following), (1, last, prev))
+    halo = (0, 2)
+
+    def edge(side):
+        j, slot, device = ends[side]
+        return pltpu.make_async_remote_copy(
+            dens.at[j - 1], mine.at[slot], edge_send.at[side], edge_recv.at[side],
+            device_id=device, device_id_type=MESH)
+
+    def relay(side):
+        source = hosted.at[pl.ds(0, pair_slots)] if side == 0 else theirs.at[1]
+        return pltpu.make_async_remote_copy(
+            source, theirs.at[halo[side]], relay_send.at[side], relay_recv.at[side],
+            device_id=ends[side][2], device_id_type=MESH)
+
+    reach = (ring // 2, ring - 1 - ring // 2)
+
+    def flag_hop(side, k):
+        source = k - 1 if side == 0 else lax.rem(ring - k + 1, ring)
+        target = k if side == 0 else ring - k
+        return pltpu.make_async_remote_copy(
+            flags.at[source], flags.at[target], flag_send.at[side, k - 1], flag_recv.at[side, k - 1],
+            device_id=ends[side][2], device_id_type=MESH)
+
+    z, r = lax.axis_index("depth"), lax.axis_index("row")
+    row_count = lax.axis_size("row")
+
+    def greet(semaphore, device):
+        pl.semaphore_signal(semaphore, inc=1, device_id=device, device_id_type=MESH)
+
+    def along(step):
+        return {"depth": z + step}
+
+    def beside(step):
+        return {"row": lax.rem(r + step + row_count, row_count)}
+
+    barrier = pltpu.get_barrier_semaphore()
+    greet(barrier, peer)
+
+    @pl.when(z > 0)
+    def _():
+        greet(barrier, along(-1))
+
+    @pl.when(z < depth - 1)
+    def _():
+        greet(barrier, along(1))
+
+    @pl.when(z == 0)
+    def _():
+        greet(barrier, beside(-1))
+        greet(barrier, beside(1))
+
+    own_bits = pltpu.make_async_copy(pattern, bits, bits_sem)
+    own_bits.start()
+    own_flags = pltpu.make_async_copy(pattern, flags.at[0], flag_sem)
+    own_flags.start()
+    for i in range(GUEST):
+        own_guest(i).start()
+    own(pairs).start()
+
+    @pl.loop(1, pairs)
+    def _(j):
+        own(j).start()
+
+    near = jnp.where(z == 0, 2, 1) + jnp.where(z < depth - 1, 1, 0)
+    pl.semaphore_wait(barrier, 1 + near)
+
+    across_first.start()
+
+    @pl.when(z > 0)
+    def _():
+        pl.semaphore_wait(up, 1)
+
+    @pl.when(z < depth - 1)
+    def _():
+        greet(up, along(1))
+
+    @pl.when(z < depth - 2)
+    def _():
+        pl.semaphore_wait(down, 1)
+
+    @pl.when((z > 0) & (z <= depth - 2))
+    def _():
+        greet(down, along(-1))
+
+    @pl.when(z == 0)
+    def _():
+        greet(corner, beside(1))
+        pl.semaphore_wait(corner, 1)
+
+    own_flags.wait()
+    for side in (0, 1):
+        flag_hop(side, 1).start()
+        edge(side).start()
+
+    own_bits.wait()
+
+    def active(j, q):
+        return bits[q % WIDE, 2 * (j - 1) + q // WIDE]
+
+    following_guest = room
+    hole[room] = room
+    hole[room + 1] = room
+    for n in reversed(range(room)):
+        used = active(first_guest + n // pair_slots, n % pair_slots)
+        following_guest = jnp.where(used > 0, n, following_guest)
+        hole[n] = following_guest
+    guest = hole[0]
+    for k in range(room):
+        queue[k] = jnp.minimum(guest, room - 1)
+        guest = hole[guest + 1]
+    queue[room] = room - 1
+
+    def fill(j, count, taken):
+        for q in range(count):
+            used = active(j, q)
+            block_in = guests[queue[taken]]
+            mine[j, q] = jnp.where(used > 0, mine[j, q], block_in)
+            taken = jnp.minimum(taken + 1 - used, room)
+        return taken
+
+    for i in range(GUEST):
+        own_guest(i).wait()
+    own(pairs).wait()
+    taken = fill(pairs, pair_slots, jnp.int32(0))
+    own(1).wait()
+    own(2).wait()
+    taken = fill(2, pair_slots, taken)
+    across_last.start()
+
+    def prepare(j, taken):
+        own(j).wait()
+        taken = fill(j, pair_slots, taken)
+        across(j - 1).start()
+        return taken
+
+    taken = lax.fori_loop(3, tail, prepare, taken)
+    own(tail).wait()
+    fill(tail, WIDE, taken)
+    across(tail - 1).start()
+
+    @pl.loop(tail + 1, pairs)
+    def _(j):
+        own(j).wait()
+
+    hole[hosts] = hosts
+    hole[hosts + 1] = hosts
+
+    def scan(j, base, count, free):
+        for q in reversed(range(count)):
+            free = jnp.where(active(j, q) > 0, free, base + q)
+            hole[base + q] = free
+        return free
+
+    free = scan(tail, (tail - 1) * pair_slots, WIDE, jnp.int32(hosts))
+
+    def scan_pair(i, free):
+        j = tail - 1 - i
+        return scan(j, (j - 1) * pair_slots, pair_slots, free)
+
+    free = lax.fori_loop(0, tail - 2, scan_pair, free)
+    spot = scan(pairs, 0, pair_slots, free)
+    across_half.start()
+    across_end.start()
+    for k in range(room):
+        queue[k] = jnp.minimum(spot, hosts - 1)
+        spot = hole[spot + 1]
+    queue[room] = hosts - 1
+    rank = jnp.int32(0)
+    for n in range(room):
+        place_of[n] = queue[rank]
+        rank = rank + active(first_guest + n // pair_slots, n % pair_slots)
+
+    def expand(which, i, j):
+        lane = lax.broadcasted_iota(jnp.int32, flags.shape[1:], 1)
+        for p in range(2):
+            picked = jnp.where(lane == i + p, flags[which], 0).astype(jnp.float32)
+            spread = jnp.broadcast_to(jnp.sum(picked, axis=1, keepdims=True), (WIDE, block))
+            for s in range(WIDE):
+                masks[j, p:p + 1, (p + s) * block:(p + s + 1) * block] = spread[s:s + 1]
+            empty = slice(0, block) if p else slice(WIDE * block, SLOTS * block)
+            masks[j, p:p + 1, empty] = jnp.zeros((1, block), jnp.float32)
+
+    def convert(j, other, rows=(0, 1)):
+        for p in rows:
+            for s in range(WIDE):
+                slot = p + s
+                lanes = slice(slot * block, (slot + 1) * block)
+                factor = masks[j, p:p + 1, lanes]
+                for c, value in ((me, mine[j, p * WIDE + s]), (1 - me, other(p * WIDE + s))):
+                    a, b = split(value * factor)
+                    at = pl.ds(pl.multiple_of(p * block + c * h, h), h)
+                    high[j, at, lanes] = a
+                    low[j, at, lanes] = b
+            empty = slice(0, block) if p else slice(WIDE * block, SLOTS * block)
+            nothing = jnp.zeros((block, block), jnp.bfloat16)
+            high[j, p * block:(p + 1) * block, empty] = nothing
+            low[j, p * block:(p + 1) * block, empty] = nothing
+
+    def arrived(j):
+        return lambda q: hosted[(j - 1) * pair_slots + q]
+
+    def direct(i):
+        return lambda q: theirs[i, q]
+
+    def visiting(j):
+        return lambda q: hosted[place_of[(j - first_guest) * pair_slots + q]]
+
+    product, own_rows, compute = products(block, h, me, masks, high, low, early)
+
+    @pl.loop(1, pairs + 1)
+    def _(j):
+        expand(0, 2 * (j - 1), j)
+
+    for side in (0, 1):
+        flag_hop(side, 1).wait_recv()
+    for side in (0, 1):
+        if reach[side] > 1:
+            flag_hop(side, 2).start()
+    expand(1, 2 * (pairs - 1), 0)
+    expand(ring - 1, 0, last)
+
+    across_first.wait_recv()
+    relay(1).start()
+    convert(1, direct(1))
+    across_last.wait_recv()
+    relay(0).start()
+    convert(pairs, lambda q: hosted[q])
+    for side in (0, 1):
+        edge(side).wait_recv()
+        relay(side).wait_recv()
+        convert(ends[side][1], direct(halo[side]))
+
+    turns = tail - 2
+    each = -(-(reach[0] - 1) // turns)
+
+    def pass_on(side, k):
+        @pl.when(k <= reach[side])
+        def _():
+            flag_hop(side, k).wait_recv()
+
+        @pl.when(k + 1 <= reach[side])
+        def _():
+            flag_hop(side, k + 1).start()
+
+    @pl.loop(2, tail)
+    def _(j):
+        for u in range(each):
+            for side in (0, 1):
+                pass_on(side, (j - 2) * each + u + 2)
+        across(j).wait_recv()
+        convert(j, arrived(j))
+        compute(j - 1, j - 2)
+
+    across_half.wait_recv()
+    for j in range(first_guest, pairs):
+        convert(j, visiting(j))
+    for i, j in enumerate(range(first_guest + 1, pairs + 1)):
+        compute(j, tail - 2 + i)
+    convert(tail, arrived(tail), (0,))
+
+    def local_rows(j):
+        rows = []
+        for p in range(2):
+            blocks = [mine[j, p * WIDE + s] for s in range(WIDE)]
+            empty = [jnp.zeros((h, block), jnp.float32)]
+            row = jnp.concatenate(empty + blocks if p else blocks + empty, axis=1)
+            rows.append(row * masks[j, p:p + 1, :])
+        return split(jnp.concatenate(rows, axis=0))
+
+    for i in range(LATE):
+        j = tail - 1 + i
+        a, b = local_rows(j) if i == 1 else (own_rows(high, j), own_rows(low, j))
+        begun[i] = product(j, a, b, BEFORE[i])
+
+    lane = lax.broadcasted_iota(jnp.int32, flags.shape[1:], 1)
+    pooled = (lane >= 2) & (lane != 2 * tail - 1)
+    most = jnp.zeros((1, 1), jnp.float32)
+    for k in range(ring):
+        counted = jnp.where(pooled, flags[k], 0).astype(jnp.float32)
+        total = jnp.sum(jnp.sum(counted, axis=1, keepdims=True), axis=0, keepdims=True)
+        most = jnp.maximum(most, total)
+    over[0] = jnp.sum(jnp.where(most > hosts, 1, 0))
+
+    for side in (0, 1):
+        edge(side).wait_send()
+        relay(side).wait_send()
+
+        @pl.loop(1, reach[side] + 1)
+        def _(k):
+            flag_hop(side, k).wait_send()
+
+    across_end.wait_recv()
+    convert(tail, direct(3), (1,))
+    across_first.wait_send()
+    across_last.wait_send()
+    across_half.wait_send()
+    across_end.wait_send()
+
+    @pl.loop(2, tail)
+    def _(j):
+        across(j).wait_send()
+
+
+DMA = pltpu.SemaphoreType.DMA
+IN_VMEM = pl.BlockSpec(memory_space=pltpu.VMEM)
+
+
+def results(pairs, wide, h, block):
+    width = SLOTS * block
+    return [
+        pltpu.VMEM((pairs + 2, 8, width), jnp.float32),
+        pltpu.VMEM((pairs + 2, 2 * block, width), jnp.bfloat16),
+        pltpu.VMEM((pairs + 2, 2 * block, width), jnp.bfloat16),
+        pltpu.VMEM((pairs - LATE, 2, wide, h, block), jnp.float32),
+        pltpu.VMEM((LATE, 2 * h, width), jnp.float32),
+    ]
+
+
+def in_hbm(*arrays):
+    return (pltpu.with_memory_space_constraint(x, pltpu.HBM) for x in arrays)
+
+
+def finished(first_late, held, pairs, wide, h, block):
+    return pl.pallas_call(
+        functools.partial(finish, first_late),
+        out_shape=pltpu.HBM((pairs, 2, wide, h, block), jnp.float32),
+        in_specs=[IN_VMEM] * 5,
+        out_specs=pl.BlockSpec(memory_space=pltpu.HBM),
+        scratch_shapes=[
+            pltpu.VMEM((LATE, 2, wide, h, block), jnp.float32),
+            DMA((2,)),
+            DMA((LATE,)),
+        ],
+        compiler_params=pltpu.CompilerParams(vmem_limit_bytes=16 << 20),
+    )(*held)
+
+
+def dense(cols, ring, density, pattern):
     rows, wide, h, block = density.shape
     pairs = rows // 2
     paired = density.reshape(pairs, 2, wide, h, block)
-    width = SLOTS * block
-    dma = pltpu.SemaphoreType.DMA
-    vmem = pl.BlockSpec(memory_space=pltpu.VMEM)
     held = pl.pallas_call(
-        functools.partial(kernel, cols, ring),
-        out_shape=[
-            pltpu.VMEM((pairs + 2, 8, width), jnp.float32),
-            pltpu.VMEM((pairs + 2, 2 * block, width), jnp.bfloat16),
-            pltpu.VMEM((pairs + 2, 2 * block, width), jnp.bfloat16),
-            pltpu.VMEM((pairs - LATE,) + paired.shape[1:], jnp.float32),
-            pltpu.VMEM((LATE, 2 * h, width), jnp.float32),
-        ],
+        functools.partial(dense_kernel, cols, ring),
+        out_shape=results(pairs, wide, h, block),
         in_specs=[pl.BlockSpec(memory_space=pltpu.HBM)] * 2,
-        out_specs=[vmem] * 5,
+        out_specs=[IN_VMEM] * 5,
         scratch_shapes=[
             pltpu.VMEM((cols, pairs + 2, 2, wide, h, block), jnp.float32),
             pltpu.VMEM((3, wide, rows), jnp.int32),
-            dma((pairs,)),
-            dma,
-            dma((cols - 1, pairs)),
-            dma((cols - 1, pairs)),
-            dma((2,)),
-            dma((2,)),
-            dma((2, cols - 1)),
-            dma((2, cols - 1)),
-            dma((2,)),
-            dma((2,)),
+            DMA((pairs,)),
+            DMA,
+            DMA((cols - 1, pairs)),
+            DMA((cols - 1, pairs)),
+            DMA((2,)),
+            DMA((2,)),
+            DMA((2, cols - 1)),
+            DMA((2, cols - 1)),
+            DMA((2,)),
+            DMA((2,)),
             pltpu.SemaphoreType.REGULAR,
             pltpu.SemaphoreType.REGULAR,
             pltpu.SemaphoreType.REGULAR,
         ],
         compiler_params=pltpu.CompilerParams(
             collective_id=0, has_side_effects=True, vmem_limit_bytes=42 << 20),
-    )(*(pltpu.with_memory_space_constraint(x, pltpu.HBM) for x in (paired, pattern.T)))
-    out = pl.pallas_call(
-        finish,
-        out_shape=jax.ShapeDtypeStruct(paired.shape, jnp.float32),
-        in_specs=[vmem] * 5,
-        out_specs=pl.BlockSpec(memory_space=pltpu.HBM),
+    )(*in_hbm(paired, pattern.T))
+    out = finished(pairs - LATE + 1, held, pairs, wide, h, block)
+    return out.reshape(density.shape)
+
+
+def sparse(ring, density, pattern):
+    rows, wide, h, block = density.shape
+    pairs = rows // 2
+    paired = density.reshape(pairs, 2 * wide, h, block)
+    tail = pairs - GUEST - 1
+    hosts = (tail - 1) * 2 * wide + wide
+    room = GUEST * 2 * wide
+    *held, over = pl.pallas_call(
+        functools.partial(sparse_kernel, ring),
+        out_shape=results(pairs, wide, h, block) + [jax.ShapeDtypeStruct((1,), jnp.int32)],
+        in_specs=[pl.BlockSpec(memory_space=pltpu.HBM)] * 2,
+        out_specs=[IN_VMEM] * 5 + [pl.BlockSpec(memory_space=pltpu.SMEM)],
         scratch_shapes=[
-            pltpu.VMEM((LATE,) + paired.shape[1:], jnp.float32),
-            dma,
-            dma((LATE,)),
+            pltpu.VMEM((pairs + 2, 2 * wide, h, block), jnp.float32),
+            pltpu.VMEM((4, 2 * wide, h, block), jnp.float32),
+            pltpu.VMEM((hosts, h, block), jnp.float32),
+            pltpu.VMEM((room, h, block), jnp.float32),
+            pltpu.VMEM((ring, wide, rows), jnp.int32),
+            pltpu.SMEM((wide, rows), jnp.int32),
+            pltpu.SMEM((room + 1,), jnp.int32),
+            pltpu.SMEM((hosts + 2,), jnp.int32),
+            pltpu.SMEM((room,), jnp.int32),
+            DMA((pairs,)),
+            DMA((GUEST,)),
+            DMA,
+            DMA,
+            DMA((tail + 2,)),
+            DMA((tail + 2,)),
+            DMA((2,)),
+            DMA((2,)),
+            DMA((2,)),
+            DMA((2,)),
+            DMA((2, ring // 2)),
+            DMA((2, ring // 2)),
+            pltpu.SemaphoreType.REGULAR,
+            pltpu.SemaphoreType.REGULAR,
+            pltpu.SemaphoreType.REGULAR,
         ],
-        compiler_params=pltpu.CompilerParams(vmem_limit_bytes=16 << 20),
-    )(*held)
-    return out.reshape(density.shape)
+        compiler_params=pltpu.CompilerParams(
+            collective_id=1, has_side_effects=True, vmem_limit_bytes=40 << 20),
+    )(*in_hbm(paired, pattern.T))
+
+    def done(density, pattern, *held):
+        return finished(tail - 1, held, pairs, wide, h, block).reshape(density.shape)
+
+    def again(density, pattern, *held):
+        return dense(2, ring, density, pattern)
+
+    return lax.cond(over[0] > 0, again, done, density, pattern, *held)
+
+
+def shards(cols, ring, density, pattern):
+    if cols == 2 and density.shape[0] >= 16:
+        return sparse(ring, density, pattern)
+    return dense(cols, ring, density, pattern)
 
 
 def solution(mesh):

time: 121 us -> 109 us (0.901)
  Pallas kernels: 121 us -> 108 us
    pallas_call x2, Pallas kernels: 121 us -> 108 us  [the longest x1 105 us: sparse(): pl.pallas_call(functools.partial(sparse_kernel, ring), out_shape=results(...]
where the time goes in v1:
time: 109 us
  Pallas kernels  108 us (99%)
    pallas_call x1, Pallas kernels, sparse(): pl.pallas_call(functools.partial(sparse_kernel, ring), out_shape=results(...  105 us
    pallas_call x1, Pallas kernels, finished(): pl.pallas_call(functools.partial(finish, first_late), out_shape=pltpu.HBM...  2.47 us

profile of v1, /device:TPU:0, one launch (start us, length us, event | category | flops | bytes accessed | tf_op | source)
XLA Modules:
  0.0 108.6 jit_solution(8240711057038442451)
XLA Ops:
  0.0 105.5 %shard_map.30 = (f32[18,8,768]{2,1,0:T(8,128)S(1)}, bf16[18,256,768]{2,1,0:T(8,128)(2,1)S(1)}, bf16[18,256,768]{2,1,0:T(8,128)(2,1)S(1)}, f32[13,2,5,64,128]{4,3...) custom-call(f32[16,10,64,128]{3,2,1,0:T(8,128)} %bitcast.7, s32[5,32]{1,0:T(8,128)} %bitcast.11), custom_call_target="tpu_custom_call" | custom-call | tf_op jit(solution)/shard_map/pallas_call | solution.py:737
  106.1 2.5 %conditional.1 = (f32[32,5,64,128]{3,2,1,0:T(8,128)}) conditional(s32[]{:T(128)} %bitcast.6, (f32[18,8,768]{2,1,0:T(8,128)S(1)}, bf16[18,256,768]{2,1,0:T(8,128)(2,1)S(1)}, bf16[18,256,768]{2,1,0:T(8,128)(2,1)S(1)}, f32[13,2,5,64,128]{4,3,2,1,0:T(8,128)S(1)}, f32[3,128,768]{2,1,0:T(8,128)S(1)}) %tuple.11, (f32[32,5,64,128]{3,2,1,0:T(8,128)}, ...), branch_computations={%region_0.0_spmd, %region_1.0_spmd} | conditional | bytes 8 | solution.py:778
  106.1 2.5 %branch_0_fun.1 = f32[16,2,5,64,128]{4,3,2,1,0:T(8,128)} custom-call(f32[18,8,768]{2,1,0:T(8,128)S(1)} %get-tuple-element.22.masks, bf16[18,256,768]{2,1,0:T(8,128)(2,1)S(1)} %get-tuple-element.23.high, bf16[18,256,768]{2,1,0:T(8,128)(2,1)S(1)} %get-tuple-element.24.low, f32[13,2,5,64,128]{4,3,2,1,0:T(8,128)S(1)} %get-tuple-element.25.early, ...), custom_call_target="tpu_custom_call" | custom-call | tf_op jit(solution)/shard_map/cond/branch_0_fun/pallas_call | solution.py:683

commit v2 on v1

--- a/solution.py
+++ b/solution.py
@@ -308,22 +308,29 @@
             across(s, j).wait_send()
 
 
-GUEST = 2
-
-
-def sparse_kernel(ring, dens, pattern, masks, high, low, early, begun, over,
-                  mine, theirs, hosted, guests, flags, bits, queue, hole, place_of,
+EXTRA = 4
+GUEST = 3
+SHARED = 6
+
+
+def sparse_kernel(ring, rows_across, dens, pattern, masks, high, low, early, begun, over,
+                  mine, theirs, stage, hosted, passed, guests, fellows, flags, fellow_flags,
+                  bits, word, need, chain, queue, spot, place_own, place_fellow, from_fellow, excess, spare,
                   local_sem, guest_sem, flag_sem, bits_sem, send_sem, recv_sem, edge_send, edge_recv,
-                  relay_send, relay_recv, flag_send, flag_recv, up, down, corner):
+                  relay_send, relay_recv, flag_send, flag_recv, fellow_send, fellow_recv,
+                  pass_send, pass_recv, up, down, corner):
     pairs, pair_slots, h, block = dens.shape
+    rows = 2 * pairs
     last = pairs + 1
     first_guest = pairs - GUEST
     tail = first_guest - 1
-    room = guests.shape[0]
+    shared = tail - SHARED
+    room = guests.shape[0] - EXTRA
     hosts = hosted.shape[0]
     me = lax.axis_index("col")
     depth = lax.axis_size("depth")
-    place = lax.axis_index("row") * depth + lax.axis_index("depth")
+    z, r = lax.axis_index("depth"), lax.axis_index("row")
+    place = r * depth + z
 
     def on_ring(shift):
         at = lax.rem(place + shift + ring, ring)
@@ -331,57 +338,75 @@
 
     prev, following = on_ring(-1), on_ring(1)
     peer = {"col": 1 - me}
+    fellow = {"row": r + 1 - 2 * lax.rem(r, 2)}
+
+    def remote(source, target, send, recv, device):
+        return pltpu.make_async_remote_copy(
+            source, target, send, recv, device_id=device, device_id_type=MESH)
 
     def own(j):
         return pltpu.make_async_copy(dens.at[j - 1], mine.at[j], local_sem.at[j - 1])
 
+    def guest_pair(i):
+        return pl.ds(i * pair_slots, pair_slots)
+
     def own_guest(i):
         return pltpu.make_async_copy(
-            dens.at[first_guest - 1 + i], guests.at[pl.ds(i * pair_slots, pair_slots)], guest_sem.at[i])
+            dens.at[first_guest - 1 + i], guests.at[guest_pair(i)], guest_sem.at[i])
+
+    def fellow_guest(i):
+        return remote(dens.at[first_guest - 1 + i], fellows.at[guest_pair(i)],
+                      fellow_send.at[i], fellow_recv.at[i], fellow)
+
+    fellow_pattern = remote(pattern, fellow_flags, fellow_send.at[GUEST], fellow_recv.at[GUEST], fellow)
+
+    def host(j):
+        return j * pair_slots - WIDE
 
     def crossing(source, target, n):
-        return pltpu.make_async_remote_copy(
-            source, target, send_sem.at[n], recv_sem.at[n], device_id=peer, device_id_type=MESH)
-
-    def at_host(j):
-        return pl.ds((j - 1) * pair_slots, pair_slots)
+        return remote(source, target, send_sem.at[n], recv_sem.at[n], peer)
+
+    def staged(start, size, n):
+        return crossing(stage.at[pl.ds(start, size)], hosted.at[pl.ds(start, size)], n)
 
     def across(j):
-        return crossing(mine.at[j], hosted.at[at_host(j)], j)
-
-    across_first = crossing(dens.at[0], theirs.at[1], 1)
-    across_last = crossing(mine.at[pairs], hosted.at[pl.ds(0, pair_slots)], 0)
-    half_host = pl.ds((tail - 1) * pair_slots, WIDE)
-    across_half = crossing(mine.at[tail, pl.ds(0, WIDE)], hosted.at[half_host], tail)
+        return staged(host(j), pair_slots, j)
+
+    across_first = crossing(dens.at[0, pl.ds(0, WIDE)], theirs.at[1, pl.ds(0, WIDE)], 0)
+    across_second = staged(0, WIDE, tail + 1)
+    across_last = staged(host(1), pair_slots, 1)
+    across_half = staged(host(tail), WIDE, tail)
+    extra_at = pl.ds(pair_slots - EXTRA, EXTRA)
+    across_extra = crossing(dens.at[pairs - 2, extra_at], theirs.at[4, extra_at], tail + 2)
     across_end = crossing(
-        dens.at[tail - 1, pl.ds(WIDE, WIDE)], theirs.at[3, pl.ds(WIDE, WIDE)], tail + 1)
+        dens.at[tail - 1, pl.ds(WIDE, WIDE)], theirs.at[3, pl.ds(WIDE, WIDE)], tail + 3)
 
     ends = ((pairs, 0, following), (1, last, prev))
     halo = (0, 2)
 
     def edge(side):
         j, slot, device = ends[side]
-        return pltpu.make_async_remote_copy(
-            dens.at[j - 1], mine.at[slot], edge_send.at[side], edge_recv.at[side],
-            device_id=device, device_id_type=MESH)
-
-    def relay(side):
-        source = hosted.at[pl.ds(0, pair_slots)] if side == 0 else theirs.at[1]
-        return pltpu.make_async_remote_copy(
-            source, theirs.at[halo[side]], relay_send.at[side], relay_recv.at[side],
-            device_id=ends[side][2], device_id_type=MESH)
+        return remote(dens.at[j - 1], mine.at[slot], edge_send.at[side], edge_recv.at[side], device)
+
+    relay_ahead = remote(hosted.at[pl.ds(host(1), pair_slots)], theirs.at[0],
+                         relay_send.at[0], relay_recv.at[0], following)
+    relay_first = remote(theirs.at[1, pl.ds(0, WIDE)], theirs.at[2, pl.ds(0, WIDE)],
+                         relay_send.at[1], relay_recv.at[1], prev)
+    relay_second = remote(hosted.at[pl.ds(0, WIDE)], theirs.at[2, pl.ds(WIDE, WIDE)],
+                          relay_send.at[2], relay_recv.at[2], prev)
+
+    def hand_over(j):
+        at = pl.ds((j - shared) * pair_slots, pair_slots)
+        return remote(hosted.at[pl.ds(host(j), pair_slots)], passed.at[at],
+                      pass_send.at[j - shared], pass_recv.at[j - shared], fellow)
 
     reach = (ring // 2, ring - 1 - ring // 2)
 
     def flag_hop(side, k):
         source = k - 1 if side == 0 else lax.rem(ring - k + 1, ring)
         target = k if side == 0 else ring - k
-        return pltpu.make_async_remote_copy(
-            flags.at[source], flags.at[target], flag_send.at[side, k - 1], flag_recv.at[side, k - 1],
-            device_id=ends[side][2], device_id_type=MESH)
-
-    z, r = lax.axis_index("depth"), lax.axis_index("row")
-    row_count = lax.axis_size("row")
+        return remote(flags.at[source], flags.at[target],
+                      flag_send.at[side, k - 1], flag_recv.at[side, k - 1], ends[side][2])
 
     def greet(semaphore, device):
         pl.semaphore_signal(semaphore, inc=1, device_id=device, device_id_type=MESH)
@@ -390,10 +415,11 @@
         return {"depth": z + step}
 
     def beside(step):
-        return {"row": lax.rem(r + step + row_count, row_count)}
+        return {"row": lax.rem(r + step + rows_across, rows_across)}
 
     barrier = pltpu.get_barrier_semaphore()
     greet(barrier, peer)
+    greet(barrier, fellow)
 
     @pl.when(z > 0)
     def _():
@@ -408,22 +434,112 @@
         greet(barrier, beside(-1))
         greet(barrier, beside(1))
 
-    own_bits = pltpu.make_async_copy(pattern, bits, bits_sem)
+    own_bits = pltpu.make_async_copy(pattern, bits.at[0], bits_sem)
     own_bits.start()
     own_flags = pltpu.make_async_copy(pattern, flags.at[0], flag_sem)
     own_flags.start()
+    own(1).start()
     for i in range(GUEST):
         own_guest(i).start()
     own(pairs).start()
 
-    @pl.loop(1, pairs)
+    @pl.loop(2, pairs)
     def _(j):
         own(j).start()
 
     near = jnp.where(z == 0, 2, 1) + jnp.where(z < depth - 1, 1, 0)
-    pl.semaphore_wait(barrier, 1 + near)
+    pl.semaphore_wait(barrier, 2 + near)
 
     across_first.start()
+    fellow_pattern.start()
+    for i in range(GUEST):
+        fellow_guest(i).start()
+
+    own_bits.wait()
+
+    def need_rows(b):
+        def pack(row, _):
+            value = bits[b, 0, row]
+            for s in range(1, WIDE):
+                value = value | (bits[b, s, row] << s)
+            word[row] = value
+            return 0
+
+        lax.fori_loop(0, rows, pack, 0, unroll=4)
+        for row in (0, 1, rows - 2, rows - 1):
+            need[b, row] = word[row]
+
+        def keep(row, _):
+            used = jnp.int32(0)
+            for d in range(-2, 3):
+                value = word[row + d]
+                moved = value << d if d >= 0 else value >> -d
+                used = used | (moved & -((value >> (2 - d)) & 1))
+            need[b, row] = word[row] & used
+            return 0
+
+        lax.fori_loop(2, rows - 2, keep, 0, unroll=4)
+
+    def active(b, row, s):
+        return (need[b, row] >> s) & 1
+
+    def row_of(j, q):
+        return 2 * (j - 1) + q // WIDE, q % WIDE
+
+    def count(value):
+        total = value & 1
+        for s in range(1, WIDE):
+            total = total + ((value >> s) & 1)
+        return total
+
+    def holes(b, row):
+        return WIDE - count(need[b, row])
+
+    def tally(b):
+        free = holes(b, rows - 2) + holes(b, rows - 1)
+        free = lax.fori_loop(1, 2 * shared - 2, lambda row, n: n + holes(b, row), free)
+        common = lax.fori_loop(2 * shared - 2, 2 * tail - 2, lambda row, n: n + holes(b, row), jnp.int32(0))
+        end = holes(b, 2 * tail - 2)
+        free = free + common + end
+        start = 2 * first_guest - 2
+        full, part = room // WIDE, room % WIDE
+        used = jnp.int32(0)
+        for i in range(full):
+            used = used + count(need[b, start + i])
+        if part:
+            used = used + count(need[b, start + full] & ((1 << part) - 1))
+        lend = jnp.minimum(common, jnp.maximum(free - end - used, 0))
+        return used, free, lend
+
+    def list_guests(b):
+        nearest = jnp.int32(room)
+        chain[room] = nearest
+        chain[room + 1] = nearest
+        for n in reversed(range(room)):
+            nearest = jnp.where(active(b, *row_of(first_guest, n)) > 0, n, nearest)
+            chain[n] = nearest
+        for k in range(room):
+            queue[b, k] = jnp.minimum(nearest, room - 1)
+            nearest = chain[nearest + 1]
+        queue[b, room] = room - 1
+
+    def fill(j, base, slots, taken):
+        for q in slots:
+            used = active(0, *row_of(j, q))
+            visitor = guests[queue[0, taken]]
+            stage[base + q] = jnp.where(used > 0, mine[j, q], visitor)
+            taken = jnp.minimum(taken + 1 - used, room)
+        return taken
+
+    need_rows(0)
+    list_guests(0)
+    own(1).wait()
+    for i in range(GUEST):
+        own_guest(i).wait()
+    taken = fill(1, -WIDE, range(WIDE, pair_slots), jnp.int32(0))
+    own(pairs).wait()
+    across_second.start()
+    taken = fill(pairs, host(1), range(pair_slots), taken)
 
     @pl.when(z > 0)
     def _():
@@ -446,88 +562,121 @@
         greet(corner, beside(1))
         pl.semaphore_wait(corner, 1)
 
+    across_last.start()
     own_flags.wait()
     for side in (0, 1):
         flag_hop(side, 1).start()
         edge(side).start()
 
-    own_bits.wait()
-
-    def active(j, q):
-        return bits[q % WIDE, 2 * (j - 1) + q // WIDE]
-
-    following_guest = room
-    hole[room] = room
-    hole[room + 1] = room
-    for n in reversed(range(room)):
-        used = active(first_guest + n // pair_slots, n % pair_slots)
-        following_guest = jnp.where(used > 0, n, following_guest)
-        hole[n] = following_guest
-    guest = hole[0]
-    for k in range(room):
-        queue[k] = jnp.minimum(guest, room - 1)
-        guest = hole[guest + 1]
-    queue[room] = room - 1
-
-    def fill(j, count, taken):
-        for q in range(count):
-            used = active(j, q)
-            block_in = guests[queue[taken]]
-            mine[j, q] = jnp.where(used > 0, mine[j, q], block_in)
-            taken = jnp.minimum(taken + 1 - used, room)
-        return taken
-
-    for i in range(GUEST):
-        own_guest(i).wait()
-    own(pairs).wait()
-    taken = fill(pairs, pair_slots, jnp.int32(0))
-    own(1).wait()
     own(2).wait()
-    taken = fill(2, pair_slots, taken)
-    across_last.start()
+    taken = fill(2, host(2), range(pair_slots), taken)
 
     def prepare(j, taken):
         own(j).wait()
-        taken = fill(j, pair_slots, taken)
+        taken = fill(j, host(j), range(pair_slots), taken)
         across(j - 1).start()
         return taken
 
-    taken = lax.fori_loop(3, tail, prepare, taken)
+    taken = lax.fori_loop(3, shared, prepare, taken)
+
+    fellow_pattern.wait_recv()
+    fellow_bits = pltpu.make_async_copy(fellow_flags, bits.at[1], bits_sem)
+    fellow_bits.start()
+    own_used, own_free, own_lend = tally(0)
+    excess[0] = jnp.maximum(own_used - own_free, 0)
+    spare[0] = own_lend
+    fellow_bits.wait()
+    need_rows(1)
+    list_guests(1)
+    fellow_used, fellow_free, _ = tally(1)
+    for i in range(GUEST):
+        fellow_guest(i).wait_recv()
+
+    def prepare_shared(j, carry):
+        taken, lent = carry
+        own(j).wait()
+        base = host(j)
+        for q in range(pair_slots):
+            used = active(0, *row_of(j, q))
+            ours = taken < own_used
+            visitor = jnp.where(
+                ours, guests[queue[0, jnp.minimum(taken, room)]],
+                fellows[queue[1, jnp.minimum(fellow_free + lent, room)]])
+            stage[base + q] = jnp.where(used > 0, mine[j, q], visitor)
+            taken = taken + 1 - used
+            lent = lent + jnp.where(ours, 0, 1 - used)
+        across(j - 1).start()
+        return taken, lent
+
+    taken, _ = lax.fori_loop(shared, tail, prepare_shared, (taken, jnp.int32(0)))
     own(tail).wait()
-    fill(tail, WIDE, taken)
+    fill(tail, host(tail), range(WIDE), jnp.minimum(taken, room))
     across(tail - 1).start()
 
     @pl.loop(tail + 1, pairs)
     def _(j):
         own(j).wait()
 
-    hole[hosts] = hosts
-    hole[hosts + 1] = hosts
-
-    def scan(j, base, count, free):
-        for q in reversed(range(count)):
-            free = jnp.where(active(j, q) > 0, free, base + q)
-            hole[base + q] = free
+    def scan(j, base, slots, free):
+        for q in reversed(slots):
+            free = jnp.where(active(0, *row_of(j, q)) > 0, free, base + q)
+            chain[base + q] = free
         return free
-
-    free = scan(tail, (tail - 1) * pair_slots, WIDE, jnp.int32(hosts))
 
     def scan_pair(i, free):
         j = tail - 1 - i
-        return scan(j, (j - 1) * pair_slots, pair_slots, free)
-
+        return scan(j, host(j), range(pair_slots), free)
+
+    free = jnp.int32(hosts)
+    chain[hosts] = free
+    chain[hosts + 1] = free
+    free = scan(tail, host(tail), range(WIDE), free)
     free = lax.fori_loop(0, tail - 2, scan_pair, free)
-    spot = scan(pairs, 0, pair_slots, free)
+    free = scan(pairs, host(1), range(pair_slots), free)
+    free = scan(1, -WIDE, range(WIDE, pair_slots), free)
     across_half.start()
+    across_extra.start()
     across_end.start()
     for k in range(room):
-        queue[k] = jnp.minimum(spot, hosts - 1)
-        spot = hole[spot + 1]
-    queue[room] = hosts - 1
+        spot[0, k] = jnp.minimum(free, hosts - 1)
+        free = chain[free + 1]
+
+    common = passed.shape[0]
+
+    def scan_fellow(i, carry):
+        nearest, above = carry
+        j = tail - 1 - i
+        for q in reversed(range(pair_slots)):
+            hole = 1 - active(1, *row_of(j, q))
+            above = above + hole
+            lends = (hole > 0) & (fellow_free - above >= fellow_used)
+            at = (j - shared) * pair_slots + q
+            nearest = jnp.where(lends, at, nearest)
+            chain[at] = nearest
+        return nearest, above
+
+    nearest = jnp.int32(common)
+    chain[common] = nearest
+    chain[common + 1] = nearest
+    nearest, _ = lax.fori_loop(0, tail - shared, scan_fellow, (nearest, holes(1, 2 * tail - 2)))
+    for k in range(room):
+        spot[1, k] = jnp.minimum(nearest, common - 1)
+        nearest = chain[nearest + 1]
     rank = jnp.int32(0)
     for n in range(room):
-        place_of[n] = queue[rank]
-        rank = rank + active(first_guest + n // pair_slots, n % pair_slots)
+        place_own[n] = spot[0, jnp.minimum(rank, room - 1)]
+        place_fellow[n] = spot[1, jnp.clip(rank - own_free, 0, room - 1)]
+        from_fellow[n] = jnp.where(rank >= own_free, 1, 0)
+        rank = rank + active(0, *row_of(first_guest, n))
+
+    def absorb(k):
+        fetch = pltpu.make_async_copy(flags.at[k], bits.at[2], bits_sem)
+        fetch.start()
+        fetch.wait()
+        need_rows(2)
+        used, free, lend = tally(2)
+        excess[k] = jnp.maximum(used - free, 0)
+        spare[k] = lend
 
     def expand(which, i, j):
         lane = lax.broadcasted_iota(jnp.int32, flags.shape[1:], 1)
@@ -539,8 +688,8 @@
             empty = slice(0, block) if p else slice(WIDE * block, SLOTS * block)
             masks[j, p:p + 1, empty] = jnp.zeros((1, block), jnp.float32)
 
-    def convert(j, other, rows=(0, 1)):
-        for p in rows:
+    def convert(j, other, halves=(0, 1)):
+        for p in halves:
             for s in range(WIDE):
                 slot = p + s
                 lanes = slice(slot * block, (slot + 1) * block)
@@ -556,13 +705,19 @@
             low[j, p * block:(p + 1) * block, empty] = nothing
 
     def arrived(j):
-        return lambda q: hosted[(j - 1) * pair_slots + q]
+        return lambda q: hosted[host(j) + q]
 
     def direct(i):
         return lambda q: theirs[i, q]
 
     def visiting(j):
-        return lambda q: hosted[place_of[(j - first_guest) * pair_slots + q]]
+        def block_at(q):
+            n = (j - first_guest) * pair_slots + q
+            if n >= room:
+                return theirs[4, q]
+            return jnp.where(from_fellow[n] > 0, passed[place_fellow[n]], hosted[place_own[n]])
+
+        return block_at
 
     product, own_rows, compute = products(block, h, me, masks, high, low, early)
 
@@ -579,15 +734,22 @@
     expand(ring - 1, 0, last)
 
     across_first.wait_recv()
-    relay(1).start()
-    convert(1, direct(1))
+    relay_first.start()
+    across_second.wait_recv()
+    relay_second.start()
+    convert(1, lambda q: theirs[1, q] if q < WIDE else hosted[q - WIDE])
     across_last.wait_recv()
-    relay(0).start()
-    convert(pairs, lambda q: hosted[q])
-    for side in (0, 1):
-        edge(side).wait_recv()
-        relay(side).wait_recv()
-        convert(ends[side][1], direct(halo[side]))
+    relay_ahead.start()
+    convert(pairs, arrived(1))
+    absorb(1)
+    absorb(ring - 1)
+    edge(0).wait_recv()
+    relay_ahead.wait_recv()
+    convert(0, direct(0))
+    edge(1).wait_recv()
+    relay_first.wait_recv()
+    relay_second.wait_recv()
+    convert(last, direct(2))
 
     turns = tail - 2
     each = -(-(reach[0] - 1) // turns)
@@ -601,58 +763,80 @@
         def _():
             flag_hop(side, k + 1).start()
 
+        @pl.when(k <= reach[side])
+        def _():
+            absorb(k if side == 0 else ring - k)
+
     @pl.loop(2, tail)
     def _(j):
+        across(j).wait_recv()
+
+        @pl.when(j >= shared)
+        def _():
+            hand_over(j).start()
+
+        convert(j, arrived(j))
+        compute(j - 1, j - 2)
         for u in range(each):
             for side in (0, 1):
                 pass_on(side, (j - 2) * each + u + 2)
-        across(j).wait_recv()
-        convert(j, arrived(j))
-        compute(j - 1, j - 2)
-
+
+    bad = jnp.int32(0)
+    for k in range(ring):
+        there = lax.rem(place - k + ring, ring)
+        band = there // depth
+        partner = there + (1 - 2 * lax.rem(band, 2)) * depth
+        bad = bad + jnp.where(excess[k] > spare[lax.rem(place - partner + ring, ring)], 1, 0)
+    over[0] = bad
+
+    for j in range(shared, tail):
+        hand_over(j).wait_recv()
     across_half.wait_recv()
-    for j in range(first_guest, pairs):
+    for j in range(first_guest, pairs - 1):
         convert(j, visiting(j))
+    convert(tail, arrived(tail), (0,))
+    across_extra.wait_recv()
+    convert(pairs - 1, visiting(pairs - 1))
     for i, j in enumerate(range(first_guest + 1, pairs + 1)):
         compute(j, tail - 2 + i)
-    convert(tail, arrived(tail), (0,))
 
     def local_rows(j):
-        rows = []
+        parts = []
         for p in range(2):
             blocks = [mine[j, p * WIDE + s] for s in range(WIDE)]
             empty = [jnp.zeros((h, block), jnp.float32)]
             row = jnp.concatenate(empty + blocks if p else blocks + empty, axis=1)
-            rows.append(row * masks[j, p:p + 1, :])
-        return split(jnp.concatenate(rows, axis=0))
+            parts.append(row * masks[j, p:p + 1, :])
+        return split(jnp.concatenate(parts, axis=0))
 
     for i in range(LATE):
         j = tail - 1 + i
         a, b = local_rows(j) if i == 1 else (own_rows(high, j), own_rows(low, j))
         begun[i] = product(j, a, b, BEFORE[i])
 
-    lane = lax.broadcasted_iota(jnp.int32, flags.shape[1:], 1)
-    pooled = (lane >= 2) & (lane != 2 * tail - 1)
-    most = jnp.zeros((1, 1), jnp.float32)
-    for k in range(ring):
-        counted = jnp.where(pooled, flags[k], 0).astype(jnp.float32)
-        total = jnp.sum(jnp.sum(counted, axis=1, keepdims=True), axis=0, keepdims=True)
-        most = jnp.maximum(most, total)
-    over[0] = jnp.sum(jnp.where(most > hosts, 1, 0))
-
+    fellow_pattern.wait_send()
+    for i in range(GUEST):
+        fellow_guest(i).wait_send()
+    for j in range(shared, tail):
+        hand_over(j).wait_send()
     for side in (0, 1):
         edge(side).wait_send()
-        relay(side).wait_send()
 
         @pl.loop(1, reach[side] + 1)
         def _(k):
             flag_hop(side, k).wait_send()
 
+    relay_ahead.wait_send()
+    relay_first.wait_send()
+    relay_second.wait_send()
+
     across_end.wait_recv()
     convert(tail, direct(3), (1,))
     across_first.wait_send()
+    across_second.wait_send()
     across_last.wait_send()
     across_half.wait_send()
+    across_extra.wait_send()
     across_end.wait_send()
 
     @pl.loop(2, tail)
@@ -732,35 +916,53 @@
     pairs = rows // 2
     paired = density.reshape(pairs, 2 * wide, h, block)
     tail = pairs - GUEST - 1
-    hosts = (tail - 1) * 2 * wide + wide
-    room = GUEST * 2 * wide
+    hosts = tail * 2 * wide
+    entries = GUEST * 2 * wide
+    room = entries - EXTRA
+    common = SHARED * 2 * wide
+    scalars = pltpu.SMEM
     *held, over = pl.pallas_call(
-        functools.partial(sparse_kernel, ring),
+        functools.partial(sparse_kernel, ring, lax.axis_size("row")),
         out_shape=results(pairs, wide, h, block) + [jax.ShapeDtypeStruct((1,), jnp.int32)],
         in_specs=[pl.BlockSpec(memory_space=pltpu.HBM)] * 2,
         out_specs=[IN_VMEM] * 5 + [pl.BlockSpec(memory_space=pltpu.SMEM)],
         scratch_shapes=[
             pltpu.VMEM((pairs + 2, 2 * wide, h, block), jnp.float32),
-            pltpu.VMEM((4, 2 * wide, h, block), jnp.float32),
+            pltpu.VMEM((5, 2 * wide, h, block), jnp.float32),
             pltpu.VMEM((hosts, h, block), jnp.float32),
-            pltpu.VMEM((room, h, block), jnp.float32),
+            pltpu.VMEM((hosts, h, block), jnp.float32),
+            pltpu.VMEM((common, h, block), jnp.float32),
+            pltpu.VMEM((entries, h, block), jnp.float32),
+            pltpu.VMEM((entries, h, block), jnp.float32),
             pltpu.VMEM((ring, wide, rows), jnp.int32),
-            pltpu.SMEM((wide, rows), jnp.int32),
-            pltpu.SMEM((room + 1,), jnp.int32),
-            pltpu.SMEM((hosts + 2,), jnp.int32),
-            pltpu.SMEM((room,), jnp.int32),
+            pltpu.VMEM((wide, rows), jnp.int32),
+            scalars((3, wide, rows), jnp.int32),
+            scalars((rows,), jnp.int32),
+            scalars((3, rows), jnp.int32),
+            scalars((hosts + 2,), jnp.int32),
+            scalars((2, room + 1), jnp.int32),
+            scalars((2, room), jnp.int32),
+            scalars((room,), jnp.int32),
+            scalars((room,), jnp.int32),
+            scalars((room,), jnp.int32),
+            scalars((ring,), jnp.int32),
+            scalars((ring,), jnp.int32),
             DMA((pairs,)),
             DMA((GUEST,)),
             DMA,
             DMA,
-            DMA((tail + 2,)),
-            DMA((tail + 2,)),
+            DMA((tail + 4,)),
+            DMA((tail + 4,)),
             DMA((2,)),
             DMA((2,)),
-            DMA((2,)),
-            DMA((2,)),
+            DMA((3,)),
+            DMA((3,)),
             DMA((2, ring // 2)),
             DMA((2, ring // 2)),
+            DMA((GUEST + 1,)),
+            DMA((GUEST + 1,)),
+            DMA((SHARED,)),
+            DMA((SHARED,)),
             pltpu.SemaphoreType.REGULAR,
             pltpu.SemaphoreType.REGULAR,
             pltpu.SemaphoreType.REGULAR,
@@ -779,7 +981,7 @@
 
 
 def shards(cols, ring, density, pattern):
-    if cols == 2 and density.shape[0] >= 16:
+    if cols == 2 and lax.axis_size("row") % 2 == 0 and density.shape[0] >= 32:
         return sparse(ring, density, pattern)
     return dense(cols, ring, density, pattern)
 

time: 109 us -> 105 us (0.963)
  Pallas kernels: 108 us -> 104 us
    pallas_call x1, Pallas kernels: 105 us -> 102 us  [sparse(): pl.pallas_call(functools.partial(sparse_kernel, ring, lax.axis_size('row'...]
where the time goes in v2:
time: 105 us
  Pallas kernels  104 us (99%)
    pallas_call x1, Pallas kernels, sparse(): pl.pallas_call(functools.partial(sparse_kernel, ring, lax.axis_size('row'...  102 us
    pallas_call x1, Pallas kernels, finished(): pl.pallas_call(functools.partial(finish, first_late), out_shape=pltpu.HBM...  2.47 us

profile of v2, /device:TPU:0, one launch (start us, length us, event | category | flops | bytes accessed | tf_op | source)
XLA Modules:
  0.0 105.3 jit_solution(8347756602448306727)
XLA Ops:
  0.0 101.8 %shard_map.30 = (f32[18,8,768]{2,1,0:T(8,128)S(1)}, bf16[18,256,768]{2,1,0:T(8,128)(2,1)S(1)}, bf16[18,256,768]{2,1,0:T(8,128)(2,1)S(1)}, f32[13,2,5,64,128]{4,3...) custom-call(f32[16,10,64,128]{3,2,1,0:T(8,128)} %bitcast.7, s32[5,32]{1,0:T(8,128)} %bitcast.11), custom_call_target="tpu_custom_call" | custom-call | tf_op jit(solution)/shard_map/pallas_call | solution.py:924
  102.4 2.7 %conditional.1 = (f32[32,5,64,128]{3,2,1,0:T(8,128)}) conditional(s32[]{:T(128)} %bitcast.6, (f32[18,8,768]{2,1,0:T(8,128)S(1)}, bf16[18,256,768]{2,1,0:T(8,128)(2,1)S(1)}, bf16[18,256,768]{2,1,0:T(8,128)(2,1)S(1)}, f32[13,2,5,64,128]{4,3,2,1,0:T(8,128)S(1)}, f32[3,128,768]{2,1,0:T(8,128)S(1)}) %tuple.11, (f32[32,5,64,128]{3,2,1,0:T(8,128)}, ...), branch_computations={%region_0.0_spmd, %region_1.0_spmd} | conditional | bytes 8 | solution.py:980
  102.4 2.5 %branch_0_fun.1 = f32[16,2,5,64,128]{4,3,2,1,0:T(8,128)} custom-call(f32[18,8,768]{2,1,0:T(8,128)S(1)} %get-tuple-element.22.masks, bf16[18,256,768]{2,1,0:T(8,128)(2,1)S(1)} %get-tuple-element.23.high, bf16[18,256,768]{2,1,0:T(8,128)(2,1)S(1)} %get-tuple-element.24.low, f32[13,2,5,64,128]{4,3,2,1,0:T(8,128)S(1)} %get-tuple-element.25.early, ...), custom_call_target="tpu_custom_call" | custom-call | tf_op jit(solution)/shard_map/cond/branch_0_fun/pallas_call | solution.py:867

commit v3 on v2

--- a/solution.py
+++ b/solution.py
@@ -318,7 +318,7 @@
                   bits, word, need, chain, queue, spot, place_own, place_fellow, from_fellow, excess, spare,
                   local_sem, guest_sem, flag_sem, bits_sem, send_sem, recv_sem, edge_send, edge_recv,
                   relay_send, relay_recv, flag_send, flag_recv, fellow_send, fellow_recv,
-                  pass_send, pass_recv, up, down, corner):
+                  pass_send, pass_recv, ready, go):
     pairs, pair_slots, h, block = dens.shape
     rows = 2 * pairs
     last = pairs + 1
@@ -411,28 +411,13 @@
     def greet(semaphore, device):
         pl.semaphore_signal(semaphore, inc=1, device_id=device, device_id_type=MESH)
 
-    def along(step):
-        return {"depth": z + step}
-
-    def beside(step):
-        return {"row": lax.rem(r + step + rows_across, rows_across)}
-
+    core = lax.rem(r, 2)
+    hub = (me == 0) & (core == 0)
     barrier = pltpu.get_barrier_semaphore()
-    greet(barrier, peer)
-    greet(barrier, fellow)
-
-    @pl.when(z > 0)
-    def _():
-        greet(barrier, along(-1))
-
-    @pl.when(z < depth - 1)
-    def _():
-        greet(barrier, along(1))
-
-    @pl.when(z == 0)
-    def _():
-        greet(barrier, beside(-1))
-        greet(barrier, beside(1))
+
+    @pl.when(hub | (core == 1))
+    def _():
+        greet(barrier, peer)
 
     own_bits = pltpu.make_async_copy(pattern, bits.at[0], bits_sem)
     own_bits.start()
@@ -447,13 +432,23 @@
     def _(j):
         own(j).start()
 
-    near = jnp.where(z == 0, 2, 1) + jnp.where(z < depth - 1, 1, 0)
-    pl.semaphore_wait(barrier, 2 + near)
+    @pl.when((me == 1) | (core == 1))
+    def _():
+        pl.semaphore_wait(barrier, 1)
+
+    @pl.when((me == 1) & (core == 0))
+    def _():
+        greet(ready, peer)
+
+    @pl.when(hub)
+    def _():
+        pl.semaphore_wait(ready, 1)
 
     across_first.start()
-    fellow_pattern.start()
-    for i in range(GUEST):
-        fellow_guest(i).start()
+
+    @pl.when((me == 0) & (core == 1))
+    def _():
+        greet(barrier, fellow)
 
     own_bits.wait()
 
@@ -541,35 +536,9 @@
     across_second.start()
     taken = fill(pairs, host(1), range(pair_slots), taken)
 
-    @pl.when(z > 0)
-    def _():
-        pl.semaphore_wait(up, 1)
-
-    @pl.when(z < depth - 1)
-    def _():
-        greet(up, along(1))
-
-    @pl.when(z < depth - 2)
-    def _():
-        pl.semaphore_wait(down, 1)
-
-    @pl.when((z > 0) & (z <= depth - 2))
-    def _():
-        greet(down, along(-1))
-
-    @pl.when(z == 0)
-    def _():
-        greet(corner, beside(1))
-        pl.semaphore_wait(corner, 1)
-
-    across_last.start()
-    own_flags.wait()
-    for side in (0, 1):
-        flag_hop(side, 1).start()
-        edge(side).start()
-
     own(2).wait()
     taken = fill(2, host(2), range(pair_slots), taken)
+    across_last.start()
 
     def prepare(j, taken):
         own(j).wait()
@@ -578,6 +547,47 @@
         return taken
 
     taken = lax.fori_loop(3, shared, prepare, taken)
+
+    deeper = hub & (z < depth - 1)
+    further = hub & (z == 0) & (r + 2 < rows_across)
+
+    @pl.when(hub)
+    def _():
+        pl.semaphore_wait(barrier, 1 + jnp.where(deeper, 1, 0) + jnp.where(further, 1, 0))
+
+    @pl.when(hub & (z > 0))
+    def _():
+        greet(barrier, {"depth": z - 1})
+
+    @pl.when(hub & (z == 0) & (r > 0))
+    def _():
+        greet(barrier, {"row": r - 2})
+
+    @pl.when(jnp.logical_not(hub & (z == 0) & (r == 0)))
+    def _():
+        pl.semaphore_wait(go, 1)
+
+    @pl.when(deeper)
+    def _():
+        greet(go, {"depth": z + 1})
+
+    @pl.when(further)
+    def _():
+        greet(go, {"row": r + 2})
+
+    @pl.when(hub)
+    def _():
+        greet(go, peer)
+        greet(go, fellow)
+        greet(go, {"row": r + 1, "col": 1 - me})
+
+    fellow_pattern.start()
+    for i in range(GUEST):
+        fellow_guest(i).start()
+    own_flags.wait()
+    for side in (0, 1):
+        flag_hop(side, 1).start()
+        edge(side).start()
 
     fellow_pattern.wait_recv()
     fellow_bits = pltpu.make_async_copy(fellow_flags, bits.at[1], bits_sem)
@@ -965,7 +975,6 @@
             DMA((SHARED,)),
             pltpu.SemaphoreType.REGULAR,
             pltpu.SemaphoreType.REGULAR,
-            pltpu.SemaphoreType.REGULAR,
         ],
         compiler_params=pltpu.CompilerParams(
             collective_id=1, has_side_effects=True, vmem_limit_bytes=40 << 20),

time: 105 us -> 104 us (level)
    pallas_call x1, Pallas kernels: 102 us -> 100 us  [sparse(): pl.pallas_call(functools.partial(sparse_kernel, ring, lax.axis_size('row'...]
where the time goes in v3:
time: 104 us
  Pallas kernels  103 us (99%)
    pallas_call x1, Pallas kernels, sparse(): pl.pallas_call(functools.partial(sparse_kernel, ring, lax.axis_size('row'...  100 us
    pallas_call x1, Pallas kernels, finished(): pl.pallas_call(functools.partial(finish, first_late), out_shape=pltpu.HBM...  2.47 us

profile of v3, /device:TPU:0, one launch (start us, length us, event | category | flops | bytes accessed | tf_op | source)
XLA Modules:
  0.0 103.9 jit_solution(12291551085319344625)
XLA Ops:
  0.0 100.3 %shard_map.30 = (f32[18,8,768]{2,1,0:T(8,128)S(1)}, bf16[18,256,768]{2,1,0:T(8,128)(2,1)S(1)}, bf16[18,256,768]{2,1,0:T(8,128)(2,1)S(1)}, f32[13,2,5,64,128]{4,3...) custom-call(f32[16,10,64,128]{3,2,1,0:T(8,128)} %bitcast.7, s32[5,32]{1,0:T(8,128)} %bitcast.11), custom_call_target="tpu_custom_call" | custom-call | tf_op jit(solution)/shard_map/pallas_call | solution.py:934
  101.0 2.7 %conditional.1 = (f32[32,5,64,128]{3,2,1,0:T(8,128)}) conditional(s32[]{:T(128)} %bitcast.6, (f32[18,8,768]{2,1,0:T(8,128)S(1)}, bf16[18,256,768]{2,1,0:T(8,128)(2,1)S(1)}, bf16[18,256,768]{2,1,0:T(8,128)(2,1)S(1)}, f32[13,2,5,64,128]{4,3,2,1,0:T(8,128)S(1)}, f32[3,128,768]{2,1,0:T(8,128)S(1)}) %tuple.11, (f32[32,5,64,128]{3,2,1,0:T(8,128)}, ...), branch_computations={%region_0.0_spmd, %region_1.0_spmd} | conditional | bytes 8 | solution.py:989
  101.0 2.5 %branch_0_fun.1 = f32[16,2,5,64,128]{4,3,2,1,0:T(8,128)} custom-call(f32[18,8,768]{2,1,0:T(8,128)S(1)} %get-tuple-element.22.masks, bf16[18,256,768]{2,1,0:T(8,128)(2,1)S(1)} %get-tuple-element.23.high, bf16[18,256,768]{2,1,0:T(8,128)(2,1)S(1)} %get-tuple-element.24.low, f32[13,2,5,64,128]{4,3,2,1,0:T(8,128)S(1)} %get-tuple-element.25.early, ...), custom_call_target="tpu_custom_call" | custom-call | tf_op jit(solution)/shard_map/cond/branch_0_fun/pallas_call | solution.py:877

commit v4 on v3

--- a/solution.py
+++ b/solution.py
@@ -41,7 +41,7 @@
                 stacked = dot(both[:, ks], high[j + k - 1, :, lanes])
                 term = stacked[:m] + stacked[m:] + dot(a[:, ks], low[j + k - 1, :, lanes])
                 total = term if total is None else total + term
-            parts.append(total)
+            parts.append(jnp.zeros((m, two), jnp.float32) if total is None else total)
         return jnp.concatenate(parts, axis=1)
 
     def own_rows(ref, j):
@@ -308,14 +308,14 @@
             across(s, j).wait_send()
 
 
-EXTRA = 4
+EXTRA = 2
 GUEST = 3
 SHARED = 6
 
 
 def sparse_kernel(ring, rows_across, dens, pattern, masks, high, low, early, begun, over,
                   mine, theirs, stage, hosted, passed, guests, fellows, flags, fellow_flags,
-                  bits, word, need, chain, queue, spot, place_own, place_fellow, from_fellow, excess, spare,
+                  bits, word, need, chain, queue, spot, place_own, place_fellow, from_fellow, excess, spare, ahead,
                   local_sem, guest_sem, flag_sem, bits_sem, send_sem, recv_sem, edge_send, edge_recv,
                   relay_send, relay_recv, flag_send, flag_recv, fellow_send, fellow_recv,
                   pass_send, pass_recv, ready, go):
@@ -799,17 +799,6 @@
         bad = bad + jnp.where(excess[k] > spare[lax.rem(place - partner + ring, ring)], 1, 0)
     over[0] = bad
 
-    for j in range(shared, tail):
-        hand_over(j).wait_recv()
-    across_half.wait_recv()
-    for j in range(first_guest, pairs - 1):
-        convert(j, visiting(j))
-    convert(tail, arrived(tail), (0,))
-    across_extra.wait_recv()
-    convert(pairs - 1, visiting(pairs - 1))
-    for i, j in enumerate(range(first_guest + 1, pairs + 1)):
-        compute(j, tail - 2 + i)
-
     def local_rows(j):
         parts = []
         for p in range(2):
@@ -819,10 +808,28 @@
             parts.append(row * masks[j, p:p + 1, :])
         return split(jnp.concatenate(parts, axis=0))
 
-    for i in range(LATE):
-        j = tail - 1 + i
-        a, b = local_rows(j) if i == 1 else (own_rows(high, j), own_rows(low, j))
-        begun[i] = product(j, a, b, BEFORE[i])
+    def converted_rows(j):
+        return own_rows(high, j), own_rows(low, j)
+
+    begun[0] = product(tail - 1, *converted_rows(tail - 1), BEFORE[0])
+    begun[1] = product(tail, *local_rows(tail), (0,))
+    ahead[0] = product(pairs - 1, *local_rows(pairs - 1), (2,))
+    ahead[1] = product(pairs, *converted_rows(pairs), (1, 2))
+
+    for j in range(shared, tail):
+        hand_over(j).wait_recv()
+    across_half.wait_recv()
+    for j in range(first_guest, pairs - 1):
+        convert(j, visiting(j))
+    convert(tail, arrived(tail), (0,))
+    begun[1] = product(tail, *local_rows(tail), (2,), begun[1])
+    across_extra.wait_recv()
+    convert(pairs - 1, visiting(pairs - 1))
+    for j in range(first_guest + 1, pairs - 1):
+        compute(j, j - LATE - 1)
+    begun[2] = product(first_guest, *converted_rows(first_guest), BEFORE[2])
+    compute(pairs - 1, pairs - LATE - 2, (0, 1), ahead[0])
+    compute(pairs, pairs - LATE - 1, (0,), ahead[1])
 
     fellow_pattern.wait_send()
     for i in range(GUEST):
@@ -852,6 +859,70 @@
     @pl.loop(2, tail)
     def _(j):
         across(j).wait_send()
+
+
+class Patched:
+    def __init__(self, ref, fixed, first):
+        self.ref, self.fixed, self.first = ref, fixed, first
+
+    def __getitem__(self, at):
+        j = at[0] - self.first
+        if 0 <= j < self.fixed.shape[0]:
+            return self.fixed[(j,) + tuple(at[1:])]
+        return self.ref[at]
+
+
+def top_up_kernel(dens, got, send_sem, recv_sem):
+    first = dens.shape[0] - 1 - GUEST
+    peer = {"col": 1 - lax.axis_index("col")}
+    barrier = pltpu.get_barrier_semaphore()
+    pl.semaphore_signal(barrier, inc=1, device_id=peer, device_id_type=MESH)
+    pl.semaphore_wait(barrier, 1)
+
+    def across(i):
+        return pltpu.make_async_remote_copy(
+            dens.at[first + i], got.at[i], send_sem.at[i], recv_sem.at[i],
+            device_id=peer, device_id_type=MESH)
+
+    for i in range(GUEST):
+        across(i).start()
+    for i in range(GUEST):
+        across(i).wait()
+
+
+def finish_again(first_late, masks, high, low, early, begun, got, out,
+                 late, fixed_high, fixed_low, early_sem, late_sem):
+    h, block = early.shape[3], early.shape[4]
+    me = lax.axis_index("col")
+    before = first_late - 1
+    count = late.shape[0]
+    first = pltpu.make_async_copy(early.at[pl.ds(0, before)], out.at[pl.ds(0, before)], early_sem)
+    first.start()
+    first_guest = first_late + count - 1 - GUEST
+    fixed_high[...] = high[pl.ds(first_guest, GUEST)]
+    fixed_low[...] = low[pl.ds(first_guest, GUEST)]
+    for i in range(GUEST):
+        for q in range(2 * WIDE):
+            p, s = divmod(q, WIDE)
+            lanes = slice((p + s) * block, (p + s + 1) * block)
+            a, b = split(got[i, q] * masks[first_guest + i, p:p + 1, lanes])
+            at = pl.ds(pl.multiple_of(p * block + (1 - me) * h, h), h)
+            fixed_high[i, at, lanes] = a
+            fixed_low[i, at, lanes] = b
+    _, _, compute = products(block, h, me, masks, Patched(high, fixed_high, first_guest),
+                             Patched(low, fixed_low, first_guest), late)
+
+    def result(i):
+        return pltpu.make_async_copy(late.at[i], out.at[before + i], late_sem.at[i])
+
+    for i in range(count):
+        compute(first_late + i, i)
+        result(i).start()
+    first.wait()
+
+    @pl.loop(0, count)
+    def _(i):
+        result(i).wait()
 
 
 DMA = pltpu.SemaphoreType.DMA
@@ -957,6 +1028,7 @@
             scalars((room,), jnp.int32),
             scalars((ring,), jnp.int32),
             scalars((ring,), jnp.int32),
+            pltpu.VMEM((2, 2 * h, SLOTS * block), jnp.float32),
             DMA((pairs,)),
             DMA((GUEST,)),
             DMA,
@@ -980,13 +1052,36 @@
             collective_id=1, has_side_effects=True, vmem_limit_bytes=40 << 20),
     )(*in_hbm(paired, pattern.T))
 
-    def done(density, pattern, *held):
-        return finished(tail - 1, held, pairs, wide, h, block).reshape(density.shape)
-
-    def again(density, pattern, *held):
-        return dense(2, ring, density, pattern)
-
-    return lax.cond(over[0] > 0, again, done, density, pattern, *held)
+    def done(paired, *held):
+        return finished(tail - 1, held, pairs, wide, h, block)
+
+    def again(paired, *held):
+        got = pl.pallas_call(
+            top_up_kernel,
+            out_shape=pltpu.VMEM((GUEST, 2 * wide, h, block), jnp.float32),
+            in_specs=[pl.BlockSpec(memory_space=pltpu.HBM)],
+            out_specs=IN_VMEM,
+            scratch_shapes=[DMA((GUEST,)), DMA((GUEST,))],
+            compiler_params=pltpu.CompilerParams(
+                collective_id=0, has_side_effects=True, vmem_limit_bytes=8 << 20),
+        )(*in_hbm(paired))
+        count = pairs - tail + 2
+        return pl.pallas_call(
+            functools.partial(finish_again, tail - 1),
+            out_shape=pltpu.HBM((pairs, 2, wide, h, block), jnp.float32),
+            in_specs=[IN_VMEM] * 6,
+            out_specs=pl.BlockSpec(memory_space=pltpu.HBM),
+            scratch_shapes=[
+                pltpu.VMEM((count, 2, wide, h, block), jnp.float32),
+                pltpu.VMEM((GUEST, 2 * block, SLOTS * block), jnp.bfloat16),
+                pltpu.VMEM((GUEST, 2 * block, SLOTS * block), jnp.bfloat16),
+                DMA,
+                DMA((count,)),
+            ],
+            compiler_params=pltpu.CompilerParams(vmem_limit_bytes=20 << 20),
+        )(*held, got)
+
+    return lax.cond(over[0] > 0, again, done, paired, *held).reshape(density.shape)
 
 
 def shards(cols, ring, density, pattern):

time: 104 us -> 102 us (0.981)
  Pallas kernels: 103 us -> 101 us
    pallas_call x1, Pallas kernels: 100 us -> 98.5 us  [sparse(): pl.pallas_call(functools.partial(sparse_kernel, ring, lax.axis_size('row'...]
where the time goes in v4:
time: 102 us
  Pallas kernels  101 us (99%)
    pallas_call x1, Pallas kernels, sparse(): pl.pallas_call(functools.partial(sparse_kernel, ring, lax.axis_size('row'...  98.5 us
    pallas_call x1, Pallas kernels, finished(): pl.pallas_call(functools.partial(finish, first_late), out_shape=pltpu.HBM...  2.47 us

profile of v4, /device:TPU:0, one launch (start us, length us, event | category | flops | bytes accessed | tf_op | source)
XLA Modules:
  0.0 102.0 jit_solution(14861911421777201142)
XLA Ops:
  0.0 98.5 %shard_map.30 = (f32[18,8,768]{2,1,0:T(8,128)S(1)}, bf16[18,256,768]{2,1,0:T(8,128)(2,1)S(1)}, bf16[18,256,768]{2,1,0:T(8,128)(2,1)S(1)}, f32[13,2,5,64,128]{4,3...) custom-call(f32[16,10,64,128]{3,2,1,0:T(8,128)} %bitcast.5, s32[5,32]{1,0:T(8,128)} %bitcast.9), custom_call_target="tpu_custom_call" | custom-call | tf_op jit(solution)/shard_map/pallas_call | solution.py:1005
  99.1 2.7 %conditional.1 = (f32[32,5,64,128]{3,2,1,0:T(8,128)}) conditional(s32[]{:T(128)} %bitcast.4, (f32[18,8,768]{2,1,0:T(8,128)S(1)}, bf16[18,256,768]{2,1,0:T(8,128)(2,1)S(1)}, bf16[18,256,768]{2,1,0:T(8,128)(2,1)S(1)}, f32[13,2,5,64,128]{4,3,2,1,0:T(8,128)S(1)}, f32[3,128,768]{2,1,0:T(8,128)S(1)}) %tuple.13, (f32[16,10,64,128]{3,2,1,0:T(8,128)}, ...), branch_computations={%region_0.0_spmd, %region_1.0_spmd} | conditional | bytes 8 | solution.py:1084
  99.1 2.5 %branch_0_fun.1 = f32[16,2,5,64,128]{4,3,2,1,0:T(8,128)} custom-call(f32[18,8,768]{2,1,0:T(8,128)S(1)} %get-tuple-element.31.masks, bf16[18,256,768]{2,1,0:T(8,128)(2,1)S(1)} %get-tuple-element.32.high, bf16[18,256,768]{2,1,0:T(8,128)(2,1)S(1)} %get-tuple-element.33.low, f32[13,2,5,64,128]{4,3,2,1,0:T(8,128)S(1)} %get-tuple-element.34.early, ...), custom_call_target="tpu_custom_call" | custom-call | tf_op jit(solution)/shard_map/cond/branch_0_fun/pallas_call | solution.py:948

commit v5 on v4

--- a/solution.py
+++ b/solution.py
@@ -1004,7 +1004,7 @@
     scalars = pltpu.SMEM
     *held, over = pl.pallas_call(
         functools.partial(sparse_kernel, ring, lax.axis_size("row")),
-        out_shape=results(pairs, wide, h, block) + [jax.ShapeDtypeStruct((1,), jnp.int32)],
+        out_shape=results(pairs, wide, h, block) + [pltpu.SMEM((1,), jnp.int32)],
         in_specs=[pl.BlockSpec(memory_space=pltpu.HBM)] * 2,
         out_specs=[IN_VMEM] * 5 + [pl.BlockSpec(memory_space=pltpu.SMEM)],
         scratch_shapes=[
@@ -1081,7 +1081,7 @@
             compiler_params=pltpu.CompilerParams(vmem_limit_bytes=20 << 20),
         )(*held, got)
 
-    return lax.cond(over[0] > 0, again, done, paired, *held).reshape(density.shape)
+    return lax.switch(over[0], [done, again], paired, *held).reshape(density.shape)
 
 
 def shards(cols, ring, density, pattern):

time: 102 us -> 101 us (level)
  no operation moved by 1% of the time
where the time goes in v5:
time: 101 us
  Pallas kernels  100 us (99%)
    pallas_call x1, Pallas kernels, sparse(): pl.pallas_call(functools.partial(sparse_kernel, ring, lax.axis_size('row'...  98 us
    pallas_call x1, Pallas kernels, finished(): pl.pallas_call(functools.partial(finish, first_late), out_shape=pltpu.HBM...  2.47 us

profile of v5, /device:TPU:0, one launch (start us, length us, event | category | flops | bytes accessed | tf_op | source)
XLA Modules:
  0.0 100.8 jit_solution(17746976124328475260)
XLA Ops:
  0.0 98.0 %shard_map.30 = (f32[18,8,768]{2,1,0:T(8,128)S(1)}, bf16[18,256,768]{2,1,0:T(8,128)(2,1)S(1)}, bf16[18,256,768]{2,1,0:T(8,128)(2,1)S(1)}, f32[13,2,5,64,128]{4,3...) custom-call(f32[16,10,64,128]{3,2,1,0:T(8,128)} %bitcast.5, s32[5,32]{1,0:T(8,128)} %bitcast.9), custom_call_target="tpu_custom_call" | custom-call | tf_op jit(solution)/shard_map/pallas_call | solution.py:1005
  98.0 2.7 %conditional.1 = (f32[32,5,64,128]{3,2,1,0:T(8,128)}) conditional(s32[]{:T(128)} %bitcast.4, (f32[18,8,768]{2,1,0:T(8,128)S(1)}, bf16[18,256,768]{2,1,0:T(8,128)(2,1)S(1)}, bf16[18,256,768]{2,1,0:T(8,128)(2,1)S(1)}, f32[13,2,5,64,128]{4,3,2,1,0:T(8,128)S(1)}, f32[3,128,768]{2,1,0:T(8,128)S(1)}) %tuple.13, (f32[16,10,64,128]{3,2,1,0:T(8,128)}, ...), branch_computations={%region_0.0_spmd, %region_1.0_spmd} | conditional | bytes 8 | solution.py:1084
  98.0 2.5 %branch_0_fun.1 = f32[16,2,5,64,128]{4,3,2,1,0:T(8,128)} custom-call(f32[18,8,768]{2,1,0:T(8,128)S(1)} %get-tuple-element.31.masks, bf16[18,256,768]{2,1,0:T(8,128)(2,1)S(1)} %get-tuple-element.32.high, bf16[18,256,768]{2,1,0:T(8,128)(2,1)S(1)} %get-tuple-element.33.low, f32[13,2,5,64,128]{4,3,2,1,0:T(8,128)S(1)} %get-tuple-element.34.early, ...), custom_call_target="tpu_custom_call" | custom-call | tf_op jit(solution)/shard_map/cond/branch_0_fun/pallas_call | solution.py:948

commit v6 on v5

--- a/solution.py
+++ b/solution.py
@@ -308,7 +308,7 @@
             across(s, j).wait_send()
 
 
-EXTRA = 2
+EXTRA = 1
 GUEST = 3
 SHARED = 6
 
@@ -500,11 +500,13 @@
         full, part = room // WIDE, room % WIDE
         used = jnp.int32(0)
         for i in range(full):
+            if i == 2 * GUEST - 2:
+                early_used = used
             used = used + count(need[b, start + i])
         if part:
             used = used + count(need[b, start + full] & ((1 << part) - 1))
         lend = jnp.minimum(common, jnp.maximum(free - end - used, 0))
-        return used, free, lend
+        return used, free, lend, early_used
 
     def list_guests(b):
         nearest = jnp.int32(room)
@@ -592,13 +594,14 @@
     fellow_pattern.wait_recv()
     fellow_bits = pltpu.make_async_copy(fellow_flags, bits.at[1], bits_sem)
     fellow_bits.start()
-    own_used, own_free, own_lend = tally(0)
-    excess[0] = jnp.maximum(own_used - own_free, 0)
+    own_used, own_free, own_lend, own_early = tally(0)
+    excess[0, 0] = jnp.maximum(own_used - own_free, 0)
+    excess[1, 0] = jnp.maximum(own_early - own_free, 0)
     spare[0] = own_lend
     fellow_bits.wait()
     need_rows(1)
     list_guests(1)
-    fellow_used, fellow_free, _ = tally(1)
+    fellow_used, fellow_free, _, _ = tally(1)
     for i in range(GUEST):
         fellow_guest(i).wait_recv()
 
@@ -684,8 +687,9 @@
         fetch.start()
         fetch.wait()
         need_rows(2)
-        used, free, lend = tally(2)
-        excess[k] = jnp.maximum(used - free, 0)
+        used, free, lend, early_used = tally(2)
+        excess[0, k] = jnp.maximum(used - free, 0)
+        excess[1, k] = jnp.maximum(early_used - free, 0)
         spare[k] = lend
 
     def expand(which, i, j):
@@ -791,13 +795,15 @@
             for side in (0, 1):
                 pass_on(side, (j - 2) * each + u + 2)
 
-    bad = jnp.int32(0)
+    level = jnp.int32(0)
     for k in range(ring):
         there = lax.rem(place - k + ring, ring)
         band = there // depth
         partner = there + (1 - 2 * lax.rem(band, 2)) * depth
-        bad = bad + jnp.where(excess[k] > spare[lax.rem(place - partner + ring, ring)], 1, 0)
-    over[0] = bad
+        lent = spare[lax.rem(place - partner + ring, ring)]
+        level = jnp.maximum(level, jnp.where(excess[0, k] > lent, 1, 0))
+        level = jnp.maximum(level, jnp.where(excess[1, k] > lent, 2, 0))
+    over[0] = level
 
     def local_rows(j):
         parts = []
@@ -873,7 +879,8 @@
 
 
 def top_up_kernel(dens, got, send_sem, recv_sem):
-    first = dens.shape[0] - 1 - GUEST
+    count = got.shape[0]
+    first = dens.shape[0] - 1 - count
     peer = {"col": 1 - lax.axis_index("col")}
     barrier = pltpu.get_barrier_semaphore()
     pl.semaphore_signal(barrier, inc=1, device_id=peer, device_id_type=MESH)
@@ -884,9 +891,9 @@
             dens.at[first + i], got.at[i], send_sem.at[i], recv_sem.at[i],
             device_id=peer, device_id_type=MESH)
 
-    for i in range(GUEST):
+    for i in range(count):
         across(i).start()
-    for i in range(GUEST):
+    for i in range(count):
         across(i).wait()
 
 
@@ -898,10 +905,11 @@
     count = late.shape[0]
     first = pltpu.make_async_copy(early.at[pl.ds(0, before)], out.at[pl.ds(0, before)], early_sem)
     first.start()
-    first_guest = first_late + count - 1 - GUEST
-    fixed_high[...] = high[pl.ds(first_guest, GUEST)]
-    fixed_low[...] = low[pl.ds(first_guest, GUEST)]
-    for i in range(GUEST):
+    fixed = got.shape[0]
+    first_guest = first_late + count - 1 - fixed
+    fixed_high[...] = high[pl.ds(first_guest, fixed)]
+    fixed_low[...] = low[pl.ds(first_guest, fixed)]
+    for i in range(fixed):
         for q in range(2 * WIDE):
             p, s = divmod(q, WIDE)
             lanes = slice((p + s) * block, (p + s + 1) * block)
@@ -916,7 +924,10 @@
         return pltpu.make_async_copy(late.at[i], out.at[before + i], late_sem.at[i])
 
     for i in range(count):
-        compute(first_late + i, i)
+        if fixed < GUEST and i < LATE:
+            compute(first_late + i, i, AFTER[i], begun[i])
+        else:
+            compute(first_late + i, i)
         result(i).start()
     first.wait()
 
@@ -1026,7 +1037,7 @@
             scalars((room,), jnp.int32),
             scalars((room,), jnp.int32),
             scalars((room,), jnp.int32),
-            scalars((ring,), jnp.int32),
+            scalars((2, ring), jnp.int32),
             scalars((ring,), jnp.int32),
             pltpu.VMEM((2, 2 * h, SLOTS * block), jnp.float32),
             DMA((pairs,)),
@@ -1055,15 +1066,17 @@
     def done(paired, *held):
         return finished(tail - 1, held, pairs, wide, h, block)
 
-    def again(paired, *held):
+    ids = {1: 2, GUEST: 0}
+
+    def again(fixed, paired, *held):
         got = pl.pallas_call(
             top_up_kernel,
-            out_shape=pltpu.VMEM((GUEST, 2 * wide, h, block), jnp.float32),
+            out_shape=pltpu.VMEM((fixed, 2 * wide, h, block), jnp.float32),
             in_specs=[pl.BlockSpec(memory_space=pltpu.HBM)],
             out_specs=IN_VMEM,
-            scratch_shapes=[DMA((GUEST,)), DMA((GUEST,))],
+            scratch_shapes=[DMA((fixed,)), DMA((fixed,))],
             compiler_params=pltpu.CompilerParams(
-                collective_id=0, has_side_effects=True, vmem_limit_bytes=8 << 20),
+                collective_id=ids[fixed], has_side_effects=True, vmem_limit_bytes=8 << 20),
         )(*in_hbm(paired))
         count = pairs - tail + 2
         return pl.pallas_call(
@@ -1073,15 +1086,16 @@
             out_specs=pl.BlockSpec(memory_space=pltpu.HBM),
             scratch_shapes=[
                 pltpu.VMEM((count, 2, wide, h, block), jnp.float32),
-                pltpu.VMEM((GUEST, 2 * block, SLOTS * block), jnp.bfloat16),
-                pltpu.VMEM((GUEST, 2 * block, SLOTS * block), jnp.bfloat16),
+                pltpu.VMEM((fixed, 2 * block, SLOTS * block), jnp.bfloat16),
+                pltpu.VMEM((fixed, 2 * block, SLOTS * block), jnp.bfloat16),
                 DMA,
                 DMA((count,)),
             ],
             compiler_params=pltpu.CompilerParams(vmem_limit_bytes=20 << 20),
         )(*held, got)
 
-    return lax.switch(over[0], [done, again], paired, *held).reshape(density.shape)
+    branches = [done, functools.partial(again, 1), functools.partial(again, GUEST)]
+    return lax.switch(over[0], branches, paired, *held).reshape(density.shape)
 
 
 def shards(cols, ring, density, pattern):

time: 101 us -> 100 us (0.990)
  no operation moved by 1% of the time
where the time goes in v6:
time: 100 us
  Pallas kernels  99.8 us (100%)
    pallas_call x1, Pallas kernels, sparse(): pl.pallas_call(functools.partial(sparse_kernel, ring, lax.axis_size('row'...  97.3 us
    pallas_call x1, Pallas kernels, finished(): pl.pallas_call(functools.partial(finish, first_late), out_shape=pltpu.HBM...  2.47 us

profile of v6, /device:TPU:0, one launch (start us, length us, event | category | flops | bytes accessed | tf_op | source)
XLA Modules:
  0.0 100.2 jit_solution(16688542854229081508)
XLA Ops:
  0.0 97.3 %shard_map.31 = (f32[18,8,768]{2,1,0:T(8,128)S(1)}, bf16[18,256,768]{2,1,0:T(8,128)(2,1)S(1)}, bf16[18,256,768]{2,1,0:T(8,128)(2,1)S(1)}, f32[13,2,5,64,128]{4,3...) custom-call(f32[16,10,64,128]{3,2,1,0:T(8,128)} %bitcast.6, s32[5,32]{1,0:T(8,128)} %bitcast.12), custom_call_target="tpu_custom_call" | custom-call | tf_op jit(solution)/shard_map/pallas_call | solution.py:1016
  97.3 2.7 %conditional.1 = (f32[32,5,64,128]{3,2,1,0:T(8,128)}) conditional(s32[]{:T(128)} %bitcast.5, (f32[18,8,768]{2,1,0:T(8,128)S(1)}, bf16[18,256,768]{2,1,0:T(8,128)(2,1)S(1)}, bf16[18,256,768]{2,1,0:T(8,128)(2,1)S(1)}, f32[13,2,5,64,128]{4,3,2,1,0:T(8,128)S(1)}, f32[3,128,768]{2,1,0:T(8,128)S(1)}) %tuple.17, ...), branch_computations={%region_0.0_spmd, %region_1.0_spmd, %region_2.0_spmd} | conditional | bytes 8 | solution.py:1098
  97.4 2.5 %branch_0_fun.1 = f32[16,2,5,64,128]{4,3,2,1,0:T(8,128)} custom-call(f32[18,8,768]{2,1,0:T(8,128)S(1)} %get-tuple-element.44.masks, bf16[18,256,768]{2,1,0:T(8,128)(2,1)S(1)} %get-tuple-element.45.high, bf16[18,256,768]{2,1,0:T(8,128)(2,1)S(1)} %get-tuple-element.46.low, f32[13,2,5,64,128]{4,3,2,1,0:T(8,128)S(1)} %get-tuple-element.47.early, ...), custom_call_target="tpu_custom_call" | custom-call | tf_op jit(solution)/shard_map/cond/branch_0_fun/pallas_call | solution.py:959

commit v7 on v6

--- a/solution.py
+++ b/solution.py
@@ -308,7 +308,6 @@
             across(s, j).wait_send()
 
 
-EXTRA = 1
 GUEST = 3
 SHARED = 6
 
@@ -325,7 +324,7 @@
     first_guest = pairs - GUEST
     tail = first_guest - 1
     shared = tail - SHARED
-    room = guests.shape[0] - EXTRA
+    room = guests.shape[0]
     hosts = hosted.shape[0]
     me = lax.axis_index("col")
     depth = lax.axis_size("depth")
@@ -376,10 +375,8 @@
     across_second = staged(0, WIDE, tail + 1)
     across_last = staged(host(1), pair_slots, 1)
     across_half = staged(host(tail), WIDE, tail)
-    extra_at = pl.ds(pair_slots - EXTRA, EXTRA)
-    across_extra = crossing(dens.at[pairs - 2, extra_at], theirs.at[4, extra_at], tail + 2)
     across_end = crossing(
-        dens.at[tail - 1, pl.ds(WIDE, WIDE)], theirs.at[3, pl.ds(WIDE, WIDE)], tail + 3)
+        dens.at[tail - 1, pl.ds(WIDE, WIDE)], theirs.at[3, pl.ds(WIDE, WIDE)], tail + 2)
 
     ends = ((pairs, 0, following), (1, last, prev))
     halo = (0, 2)
@@ -497,14 +494,11 @@
         end = holes(b, 2 * tail - 2)
         free = free + common + end
         start = 2 * first_guest - 2
-        full, part = room // WIDE, room % WIDE
         used = jnp.int32(0)
-        for i in range(full):
+        for i in range(2 * GUEST):
             if i == 2 * GUEST - 2:
                 early_used = used
             used = used + count(need[b, start + i])
-        if part:
-            used = used + count(need[b, start + full] & ((1 << part) - 1))
         lend = jnp.minimum(common, jnp.maximum(free - end - used, 0))
         return used, free, lend, early_used
 
@@ -648,7 +642,6 @@
     free = scan(pairs, host(1), range(pair_slots), free)
     free = scan(1, -WIDE, range(WIDE, pair_slots), free)
     across_half.start()
-    across_extra.start()
     across_end.start()
     for k in range(room):
         spot[0, k] = jnp.minimum(free, hosts - 1)
@@ -702,17 +695,22 @@
             empty = slice(0, block) if p else slice(WIDE * block, SLOTS * block)
             masks[j, p:p + 1, empty] = jnp.zeros((1, block), jnp.float32)
 
-    def convert(j, other, halves=(0, 1)):
+    def convert(j, other, halves=(0, 1), ours=True):
         for p in halves:
             for s in range(WIDE):
                 slot = p + s
                 lanes = slice(slot * block, (slot + 1) * block)
                 factor = masks[j, p:p + 1, lanes]
-                for c, value in ((me, mine[j, p * WIDE + s]), (1 - me, other(p * WIDE + s))):
+                pieces = [(me, mine[j, p * WIDE + s])] if ours else []
+                if other is not None:
+                    pieces.append((1 - me, other(p * WIDE + s)))
+                for c, value in pieces:
                     a, b = split(value * factor)
                     at = pl.ds(pl.multiple_of(p * block + c * h, h), h)
                     high[j, at, lanes] = a
                     low[j, at, lanes] = b
+            if not ours:
+                continue
             empty = slice(0, block) if p else slice(WIDE * block, SLOTS * block)
             nothing = jnp.zeros((block, block), jnp.bfloat16)
             high[j, p * block:(p + 1) * block, empty] = nothing
@@ -727,8 +725,6 @@
     def visiting(j):
         def block_at(q):
             n = (j - first_guest) * pair_slots + q
-            if n >= room:
-                return theirs[4, q]
             return jnp.where(from_fellow[n] > 0, passed[place_fellow[n]], hosted[place_own[n]])
 
         return block_at
@@ -765,6 +761,23 @@
     relay_second.wait_recv()
     convert(last, direct(2))
 
+    def local_rows(j):
+        parts = []
+        for p in range(2):
+            blocks = [mine[j, p * WIDE + s] for s in range(WIDE)]
+            empty = [jnp.zeros((h, block), jnp.float32)]
+            row = jnp.concatenate(empty + blocks if p else blocks + empty, axis=1)
+            parts.append(row * masks[j, p:p + 1, :])
+        return split(jnp.concatenate(parts, axis=0))
+
+    def converted_rows(j):
+        return own_rows(high, j), own_rows(low, j)
+
+    for j in range(tail, pairs):
+        convert(j, None)
+    ahead[0] = product(pairs - 1, *local_rows(pairs - 1), (2,))
+    ahead[1] = product(pairs, *converted_rows(pairs), (1, 2))
+
     turns = tail - 2
     each = -(-(reach[0] - 1) // turns)
 
@@ -805,32 +818,17 @@
         level = jnp.maximum(level, jnp.where(excess[1, k] > lent, 2, 0))
     over[0] = level
 
-    def local_rows(j):
-        parts = []
-        for p in range(2):
-            blocks = [mine[j, p * WIDE + s] for s in range(WIDE)]
-            empty = [jnp.zeros((h, block), jnp.float32)]
-            row = jnp.concatenate(empty + blocks if p else blocks + empty, axis=1)
-            parts.append(row * masks[j, p:p + 1, :])
-        return split(jnp.concatenate(parts, axis=0))
-
-    def converted_rows(j):
-        return own_rows(high, j), own_rows(low, j)
-
     begun[0] = product(tail - 1, *converted_rows(tail - 1), BEFORE[0])
     begun[1] = product(tail, *local_rows(tail), (0,))
-    ahead[0] = product(pairs - 1, *local_rows(pairs - 1), (2,))
-    ahead[1] = product(pairs, *converted_rows(pairs), (1, 2))
 
     for j in range(shared, tail):
         hand_over(j).wait_recv()
     across_half.wait_recv()
     for j in range(first_guest, pairs - 1):
-        convert(j, visiting(j))
-    convert(tail, arrived(tail), (0,))
+        convert(j, visiting(j), ours=False)
+    convert(tail, arrived(tail), (0,), False)
     begun[1] = product(tail, *local_rows(tail), (2,), begun[1])
-    across_extra.wait_recv()
-    convert(pairs - 1, visiting(pairs - 1))
+    convert(pairs - 1, visiting(pairs - 1), ours=False)
     for j in range(first_guest + 1, pairs - 1):
         compute(j, j - LATE - 1)
     begun[2] = product(first_guest, *converted_rows(first_guest), BEFORE[2])
@@ -854,12 +852,11 @@
     relay_second.wait_send()
 
     across_end.wait_recv()
-    convert(tail, direct(3), (1,))
+    convert(tail, direct(3), (1,), False)
     across_first.wait_send()
     across_second.wait_send()
     across_last.wait_send()
     across_half.wait_send()
-    across_extra.wait_send()
     across_end.wait_send()
 
     @pl.loop(2, tail)
@@ -1009,8 +1006,7 @@
     paired = density.reshape(pairs, 2 * wide, h, block)
     tail = pairs - GUEST - 1
     hosts = tail * 2 * wide
-    entries = GUEST * 2 * wide
-    room = entries - EXTRA
+    room = GUEST * 2 * wide
     common = SHARED * 2 * wide
     scalars = pltpu.SMEM
     *held, over = pl.pallas_call(
@@ -1020,12 +1016,12 @@
         out_specs=[IN_VMEM] * 5 + [pl.BlockSpec(memory_space=pltpu.SMEM)],
         scratch_shapes=[
             pltpu.VMEM((pairs + 2, 2 * wide, h, block), jnp.float32),
-            pltpu.VMEM((5, 2 * wide, h, block), jnp.float32),
+            pltpu.VMEM((4, 2 * wide, h, block), jnp.float32),
             pltpu.VMEM((hosts, h, block), jnp.float32),
             pltpu.VMEM((hosts, h, block), jnp.float32),
             pltpu.VMEM((common, h, block), jnp.float32),
-            pltpu.VMEM((entries, h, block), jnp.float32),
-            pltpu.VMEM((entries, h, block), jnp.float32),
+            pltpu.VMEM((room, h, block), jnp.float32),
+            pltpu.VMEM((room, h, block), jnp.float32),
             pltpu.VMEM((ring, wide, rows), jnp.int32),
             pltpu.VMEM((wide, rows), jnp.int32),
             scalars((3, wide, rows), jnp.int32),
@@ -1044,8 +1040,8 @@
             DMA((GUEST,)),
             DMA,
             DMA,
-            DMA((tail + 4,)),
-            DMA((tail + 4,)),
+            DMA((tail + 3,)),
+            DMA((tail + 3,)),
             DMA((2,)),
             DMA((2,)),
             DMA((3,)),

time: 100 us -> 99.5 us (level)
  no operation moved by 1% of the time
where the time goes in v7:
time: 99.5 us; the launch traced here: 99.3 us
  Pallas kernels  98.9 us (99%)
    pallas_call x1, Pallas kernels, sparse(): pl.pallas_call(functools.partial(sparse_kernel, ring, lax.axis_size('row'...  96.4 us
    pallas_call x1, Pallas kernels, finished(): pl.pallas_call(functools.partial(finish, first_late), out_shape=pltpu.HBM...  2.47 us

profile of v7, /device:TPU:0, one launch (start us, length us, event | category | flops | bytes accessed | tf_op | source)
XLA Modules:
  0.0 99.3 jit_solution(2805382953824886720)
XLA Ops:
  0.0 96.4 %shard_map.31 = (f32[18,8,768]{2,1,0:T(8,128)S(1)}, bf16[18,256,768]{2,1,0:T(8,128)(2,1)S(1)}, bf16[18,256,768]{2,1,0:T(8,128)(2,1)S(1)}, f32[13,2,5,64,128]{4,3...) custom-call(f32[16,10,64,128]{3,2,1,0:T(8,128)} %bitcast.6, s32[5,32]{1,0:T(8,128)} %bitcast.12), custom_call_target="tpu_custom_call" | custom-call | tf_op jit(solution)/shard_map/pallas_call | solution.py:1012
  96.4 2.7 %conditional.1 = (f32[32,5,64,128]{3,2,1,0:T(8,128)}) conditional(s32[]{:T(128)} %bitcast.5, (f32[18,8,768]{2,1,0:T(8,128)S(1)}, bf16[18,256,768]{2,1,0:T(8,128)(2,1)S(1)}, bf16[18,256,768]{2,1,0:T(8,128)(2,1)S(1)}, f32[13,2,5,64,128]{4,3,2,1,0:T(8,128)S(1)}, f32[3,128,768]{2,1,0:T(8,128)S(1)}) %tuple.17, ...), branch_computations={%region_0.0_spmd, %region_1.0_spmd, %region_2.0_spmd} | conditional | bytes 8 | solution.py:1094
  96.5 2.5 %branch_0_fun.1 = f32[16,2,5,64,128]{4,3,2,1,0:T(8,128)} custom-call(f32[18,8,768]{2,1,0:T(8,128)S(1)} %get-tuple-element.44.masks, bf16[18,256,768]{2,1,0:T(8,128)(2,1)S(1)} %get-tuple-element.45.high, bf16[18,256,768]{2,1,0:T(8,128)(2,1)S(1)} %get-tuple-element.46.low, f32[13,2,5,64,128]{4,3,2,1,0:T(8,128)S(1)} %get-tuple-element.47.early, ...), custom_call_target="tpu_custom_call" | custom-call | tf_op jit(solution)/shard_map/cond/branch_0_fun/pallas_call | solution.py:956
